TPU v7x, 256 devices: a whole 4x4x8 slice. The times are simulated.
256 devices in a mesh: gx: 8 (over z), gy: 32 (over x, y, core).
Axes of the slice: x: 4, y: 4, z: 8, core: 2. Of those that a mesh axis runs over, the one named last changes fastest.
Arguments:
- permeability: float32 [3, 256, 65536], P(None, 'gx', 'gy'), may hold values from 0.03 to 1000, as said below
Outputs:
- fine_pressure: float32 [256, 65536], P('gx', 'gy')
- twin_pressure: float32 [128, 16384], P('gx', 'gy')
Inputs may be any that keep to these rules, and one draw needn't show every extreme that they name: `permeability`: positive conductivities; entry 0, 1, 2 of the first dimension is the conductivity along the grid's first, second, third dimension.
All inputs are finite; a program needn't handle non-finite values.
Results may differ from a plain program's by a relative error of at most 0.0003.
Values sent between devices are 32-bit elements; how exact they have to be, the bound alone decides.
A program may use at most 192 MiB of HBM per device.

v0:
```python
import jax
import jax.numpy as jnp
from jax import lax
from jax.sharding import PartitionSpec as P

EL = 32
ELZ = 16
MX = 4
MZ = 2
EZ = 2
PATCH_ITERS = 3
COARSE_ITERS = 2


def shifted(shard, axis, by):
    count = lax.axis_size(axis)
    return lax.ppermute(shard, axis, [(i, (i + by) % count) for i in range(count)])


def padded_2(cells, sides, width):
    for axis, dim in sides:
        count = lax.axis_size(axis)
        head = lax.slice_in_dim(cells, 0, width, axis=dim)
        tail = lax.slice_in_dim(cells, cells.shape[dim] - width, cells.shape[dim], axis=dim)
        cells = jnp.concatenate(
            [
                lax.ppermute(tail, axis, [(i, (i + 1) % count) for i in range(count)]),
                cells,
                lax.ppermute(head, axis, [((i + 1) % count, i) for i in range(count)]),
            ],
            axis=dim,
        )
    return cells


def harmonic(first, second, spacing):
    return spacing * 2.0 * first * second / (first + second)


def face_weights(conduct, width, spacing):
    weight_rows = harmonic(conduct[0][..., :-width], conduct[0][..., width:], spacing)
    weight_cols = harmonic(conduct[1][..., :-1], conduct[1][..., 1:], spacing)
    column = jnp.arange(weight_cols.shape[-1], dtype=jnp.int32) % width
    weight_cols = jnp.where(column == width - 1, jnp.zeros_like(weight_cols), weight_cols)
    weight_depth = harmonic(conduct[2][:, :-1], conduct[2][:, 1:], spacing)
    return (weight_rows, weight_cols, weight_depth)


def apply_operator(field, weights, width):
    weight_rows, weight_cols, weight_depth = weights
    flux = weight_rows * (field[..., :-width] - field[..., width:])
    result = jnp.pad(flux, ((0, 0), (0, 0), (0, 0), (0, width))) - jnp.pad(
        flux, ((0, 0), (0, 0), (0, 0), (width, 0))
    )
    flux = weight_cols * (field[..., :-1] - field[..., 1:])
    result = (
        result
        + jnp.pad(flux, ((0, 0), (0, 0), (0, 0), (0, 1)))
        - jnp.pad(flux, ((0, 0), (0, 0), (0, 0), (1, 0)))
    )
    flux = weight_depth * (field[:, :, :-1] - field[:, :, 1:])
    result = (
        result
        + jnp.pad(flux, ((0, 0), (0, 0), (0, 1), (0, 0)))
        - jnp.pad(flux, ((0, 0), (0, 0), (1, 0), (0, 0)))
    )
    return result


def interior_mask(depth, rows, width):
    level = jnp.arange(depth, dtype=jnp.int32)[:, None]
    cell = jnp.arange(rows * width, dtype=jnp.int32)[None, :]
    row_index = cell // width
    line_index = cell % width
    inside = (
        (level > 0)
        & (level < depth - 1)
        & (row_index > 0)
        & (row_index < rows - 1)
        & (line_index > 0)
        & (line_index < width - 1)
    )
    return inside.astype(jnp.float32)


def shape_functions(depth, rows, width, edge, edge_depth, margin, margin_depth):
    cell = jnp.arange(rows * width, dtype=jnp.int32)
    place_rows = ((cell // width).astype(jnp.float32) - margin + 0.5) / edge
    place_cols = ((cell % width).astype(jnp.float32) - margin + 0.5) / edge
    place_depth = (
        jnp.arange(depth, dtype=jnp.int32).astype(jnp.float32) - margin_depth + 0.5
    ) / edge_depth
    factors = []
    for basis in range(8):
        along_rows = place_rows if basis // 4 else 1.0 - place_rows
        along_cols = place_cols if basis // 2 % 2 else 1.0 - place_cols
        along_depth = place_depth if basis % 2 else 1.0 - place_depth
        factors.append(along_depth[:, None] * (along_rows * along_cols)[None, :])
    return jnp.stack(factors)[:, None]


def patch_fields(block, edge_depth, margin_depth):
    depth = edge_depth + 2 * margin_depth
    count = (block.shape[3] - 2 * margin_depth) // edge_depth
    pieces = [
        block[:, :, :, index * edge_depth : index * edge_depth + depth] for index in range(count)
    ]
    stacked = jnp.stack(pieces, axis=1)
    return jnp.transpose(stacked, (0, 1, 4, 2, 3)).reshape(
        3, count, depth, block.shape[1] * block.shape[2]
    )


def solve_column(block, edge, edge_depth, margin, margin_depth, spacing):
    rows = block.shape[1]
    width = block.shape[2]
    depth = edge_depth + 2 * margin_depth
    conduct = patch_fields(block, edge_depth, margin_depth)
    count = conduct.shape[1]
    weights = face_weights(conduct, width, spacing)
    inside = interior_mask(depth, rows, width)
    start = shape_functions(depth, rows, width, edge, edge_depth, margin, margin_depth)
    residual = -inside * apply_operator(start, weights, width)
    direction = residual
    norm_now = jnp.sum(residual * residual, axis=(2, 3), keepdims=True)
    update = jnp.zeros_like(residual)
    for step in range(PATCH_ITERS):
        image = inside * apply_operator(direction, weights, width)
        alpha = norm_now / jnp.sum(direction * image, axis=(2, 3), keepdims=True)
        update = update + alpha * direction
        residual = residual - alpha * image
        norm_next = jnp.sum(residual * residual, axis=(2, 3), keepdims=True)
        direction = residual + norm_next / norm_now * direction
        norm_now = norm_next
    solution = start + update
    local = solution.reshape(8, count, depth, rows, width)[
        :,
        :,
        margin_depth : margin_depth + edge_depth,
        margin : margin + edge,
        margin : margin + edge,
    ]
    local = local.reshape(8, count, edge_depth, edge * edge)
    element_conduct = conduct.reshape(3, count, depth, rows, width)[
        :,
        :,
        margin_depth : margin_depth + edge_depth,
        margin : margin + edge,
        margin : margin + edge,
    ]
    element_conduct = element_conduct.reshape(3, count, edge_depth, edge * edge)
    inner_rows, inner_cols, inner_depth = face_weights(element_conduct, edge, spacing)
    jump = local[..., :-edge] - local[..., edge:]
    stiffness = jnp.einsum(
        "aezn,bezn->eab", jump * inner_rows, jump, precision=lax.Precision.HIGHEST
    )
    jump = local[..., :-1] - local[..., 1:]
    stiffness = stiffness + jnp.einsum(
        "aezn,bezn->eab", jump * inner_cols, jump, precision=lax.Precision.HIGHEST
    )
    jump = local[:, :, :-1] - local[:, :, 1:]
    stiffness = stiffness + jnp.einsum(
        "aezn,bezn->eab", jump * inner_depth, jump, precision=lax.Precision.HIGHEST
    )
    return (local, stiffness)


def coarsen(block):
    comps, rows, width, depth = block.shape
    grouped = block.reshape(comps, rows // 2, 2, width // 2, 2, depth // 2, 2)
    return 0.125 * jnp.sum(grouped, axis=(2, 4, 6))


def corner_stack(corner_first, corner_rows, corner_cols, corner_both, count):
    table = [[corner_first, corner_cols], [corner_rows, corner_both]]
    values = []
    for basis in range(8):
        lift = basis % 2
        values.append(table[basis // 4][basis // 2 % 2][..., lift : lift + count])
    return jnp.stack(values, axis=-1)


def spread(values):
    parts = [[None, None], [None, None]]
    for basis in range(8):
        lift = basis % 2
        widths = [(0, 0)] * (values.ndim - 2) + [(lift, 1 - lift)]
        padded = jnp.pad(values[..., basis], widths)
        first = basis // 4
        second = basis // 2 % 2
        if parts[first][second] is None:
            parts[first][second] = padded
        else:
            parts[first][second] = parts[first][second] + padded
    return parts


def pressure_tile(local, weights, edge):
    combined = jnp.sum(jnp.transpose(weights)[:, :, None, None] * local, axis=0)
    count = combined.shape[0]
    depth = combined.shape[1]
    return jnp.transpose(combined.reshape(count, depth, edge, edge), (2, 3, 0, 1)).reshape(
        edge, edge, count * depth
    )


def neighbours(nodes):
    next_rows = shifted(nodes, "gx", -1)
    fetched = shifted(jnp.stack([nodes[:, 0], next_rows[:, 0]]), "gy", -1)
    next_cols = jnp.concatenate([nodes[:, 1:], fetched[0][:, None]], axis=1)
    next_both = jnp.concatenate([next_rows[:, 1:], fetched[1][:, None]], axis=1)
    return (next_rows, next_cols, next_both)


def local_operator(stiffness, nodes, count):
    next_rows, next_cols, next_both = neighbours(nodes)
    element = corner_stack(nodes, next_rows, next_cols, next_both, count)
    local = jnp.einsum("lckab,lckb->lcka", stiffness, element, precision=lax.Precision.HIGHEST)
    parts = spread(local)
    col_part = parts[0][1]
    both_part = parts[1][1]
    returned = shifted(jnp.stack([col_part[:, -1], both_part[:, -1]]), "gy", 1)
    moved_cols = jnp.concatenate([returned[0][:, None], col_part[:, :-1]], axis=1)
    moved_both = jnp.concatenate([returned[1][:, None], both_part[:, :-1]], axis=1)
    across = shifted(parts[1][0] + moved_both, "gx", 1)
    return parts[0][0] + moved_cols + across


def squares(residual):
    return lax.psum(jnp.sum(residual * residual, axis=(1, 2), keepdims=True), ("gx", "gy"))


def spread_solve(stiffness, columns, count):
    level = jnp.arange(count + 1, dtype=jnp.int32)
    inside = ((level > 0) & (level < count)).astype(jnp.float32)
    boundary = jnp.broadcast_to((level == 0).astype(jnp.float32), (2, columns, count + 1))
    source = -inside * local_operator(stiffness, boundary, count)
    update = jnp.zeros_like(source)
    residual = source
    direction = source
    norm_now = squares(residual)
    for step in range(COARSE_ITERS):
        image = inside * local_operator(stiffness, direction, count)
        alpha = norm_now / lax.psum(
            jnp.sum(direction * image, axis=(1, 2), keepdims=True), ("gx", "gy")
        )
        update = update + alpha * direction
        residual = residual - alpha * image
        norm_next = squares(residual)
        direction = residual + norm_next / norm_now * direction
        norm_now = norm_next
    return boundary + update


def shards(permeability):
    depth_total = ELZ * EZ
    shaped = permeability.reshape(
        3, permeability.shape[1], permeability.shape[2] // depth_total, depth_total
    )
    rimmed = padded_2(shaped, (("gx", 1), ("gy", 2)), MX)
    half_edge = EL // 2
    columns = shaped.shape[2] // EL

    def column_work(offset):
        block = lax.dynamic_slice_in_dim(rimmed, offset, EL + 2 * MX, 2)
        fine_block = jnp.pad(block, ((0, 0), (0, 0), (0, 0), (MZ, MZ)), mode="edge")
        twin_block = coarsen(fine_block)
        fine_local, fine_stiff = solve_column(fine_block, EL, ELZ, MX, MZ, 1.0)
        twin_local, twin_stiff = solve_column(
            twin_block, half_edge, ELZ // 2, MX // 2, MZ // 2, 2.0
        )
        return (fine_local, fine_stiff, twin_local, twin_stiff)

    offsets = jnp.arange(columns, dtype=jnp.int32) * EL
    fine_local, fine_stiff, twin_local, twin_stiff = lax.map(column_work, offsets)
    stiffness = jnp.stack([fine_stiff, twin_stiff])
    count = stiffness.shape[2]
    corner_first = spread_solve(stiffness, columns, count)
    corner_rows, corner_cols, corner_both = neighbours(corner_first)
    weights = corner_stack(corner_first, corner_rows, corner_cols, corner_both, count)
    fine_tiles = [
        pressure_tile(fine_local[column], weights[0, column], EL) for column in range(columns)
    ]
    twin_tiles = [
        pressure_tile(twin_local[column], weights[1, column], half_edge)
        for column in range(columns)
    ]
    fine_pressure = jnp.concatenate(fine_tiles, axis=1)
    twin_pressure = jnp.concatenate(twin_tiles, axis=1)
    return (fine_pressure.reshape(EL, -1), twin_pressure.reshape(half_edge, -1))


def solution(mesh):
    placed = (P(None, "gx", "gy"),)
    return jax.shard_map(
        shards,
        mesh=mesh,
        in_specs=placed,
        out_specs=(P("gx", "gy"), P("gx", "gy")),
        check_vma=False,
    )
```

profile of v0, /device:TPU:1, one launch (start us, length us, event | category | flops | bytes accessed | tf_op | source)
XLA Modules:
  0.0 635.2 jit_solution(149568154038995864)
XLA Ops:
  6.1 3.9 collective-permute-start.1
  13.8 4.4 collective-permute-done.4
  27.6 2.6 collective-permute-start.3
  32.8 2.7 copy.335
  39.7 4.5 pad_maximum_fusion.3
  44.2 299.3 %while.21 = (s32[]{:T(128)}, f32[2,8,2,16,1024]{4,1,3,2,0:T(8,128)}, f32[2,2,8,8]{3,2,1,0:T(8,128)}, f32[2,8,2,8,256]{4,1,3,2,0:T(8,128)}, f32[2,2,8,8]{3,2,1,0:...) while((s32[]{:T(128)}, ...), condition=%wide.region_14.15_spmd, body=%wide.region_0.14_spmd.sunk | while | flops 130577320 | bytes 255059728 | solution.py:275
  90.3 5.9 reshape.1503
  96.2 5.7 slice.2293
  102.0 3.7 broadcast_in_dim.249
  106.8 3.9 reshape.1504
  110.7 2.9 fusion.260
  121.9 2.5 fusion.262
  126.4 3.0 fusion.264
  131.4 26.2 %reshape.1505 = f32[3,20,2,20,2,18,2]{4,3,2,1,6,5,0:T(8,128)} reshape(f32[3,40,40,36]{2,1,3,0:T(8,128)} %pad_maximum_fusion.26) | data formatting | bytes 1382400 | tf_op jit(solution)/shard_map/while/body/eval_jaxpr/reshape | solution.py:170
  157.7 19.5 %reduce_sum.329 = f32[3,20,20,18]{2,1,3,0:T(8,128)S(1)} reduce(f32[3,20,2,20,2,18,2]{4,3,2,1,6,5,0:T(8,128)} %reshape.1505, f32[]{:T(128)} %constant.340.clone.31..sunk), dimensions={2,4,6}, to_apply=%region_7.7 | reduce | flops 151200 | bytes 777604 | tf_op jit(solution)/shard_map/while/body/eval_jaxpr/reduce_sum | solution.py:171
  235.5 5.9 reshape.1503
  241.5 5.7 slice.2293
  247.2 3.7 broadcast_in_dim.249
  252.0 4.0 reshape.1504
  256.0 2.9 fusion.260
  267.2 2.5 fusion.262
  271.7 3.0 fusion.264
  276.7 26.2 %reshape.1505 = f32[3,20,2,20,2,18,2]{4,3,2,1,6,5,0:T(8,128)} reshape(f32[3,40,40,36]{2,1,3,0:T(8,128)} %pad_maximum_fusion.26) | data formatting | bytes 1382400 | tf_op jit(solution)/shard_map/while/body/eval_jaxpr/reshape | solution.py:170
  302.9 19.7 %reduce_sum.329 = f32[3,20,20,18]{2,1,3,0:T(8,128)S(1)} reduce(f32[3,20,2,20,2,18,2]{4,3,2,1,6,5,0:T(8,128)} %reshape.1505, f32[]{:T(128)} %constant.340.clone.31..sunk), dimensions={2,4,6}, to_apply=%region_7.7 | reduce | flops 151200 | bytes 777604 | tf_op jit(solution)/shard_map/while/body/eval_jaxpr/reduce_sum | solution.py:171
  344.9 7.2 %collective-permute-done.6 = f32[2,2,3]{2,1,0:T(2,128)S(1)} collective-permute-done((f32[2,2,3]{2,1,0:T(2,128)S(1)}, f32[2,2,3]{2,1,0:T(2,128)S(1)}, u32[]{:S(2)}, u32[]{:S(2)}) %collective-permute-start.6) | collective-permute-done | bytes 80 | tf_op jit(solution)/shard_map/ppermute | solution.py:17
  352.2 4.6 collective-permute-done.7
  360.1 7.4 %collective-permute-start.9 = (f32[2,2,3]{2,1,0:T(2,128)S(1)}, f32[2,2,3]{2,1,0:T(2,128)S(1)}, u32[]{:S(2)}, u32[]{:S(2)}) collective-permute-start(f32[2,2,3]{2,1,0:T(2,128)S(1)} %pad_maximum_fusion.20), channel_id=1, source_target_pairs={{0,31},{1,0},{2,1},{3,2},{4,3},{5,4},{6,5},{7,6},{8,7},{9,8},{10,9... | collective-permute-start | bytes 152 | tf_op jit(solution)/shard_map/ppermute | solution.py:17
  371.6 4.2 collective-permute-done.11
  376.6 77.9 %all-reduce.72 = (f32[2,1,1]{0,2,1:T(1,128)S(1)}, f32[2,1,1]{0,2,1:T(1,128)S(1)}) all-reduce(f32[2,1,1]{0,2,1:T(1,128)S(1)} %bitcast.449, f32[2,1,1]{0,2,1:T(1,128)S(1)} %bitcast.448), channel_id=1, replica_groups=mesh['gx'=8,'gy'=32] {'gx','gy'}, use_global_device_ids=true, to_apply=%region_16.17 | all-reduce | flops 4 | bytes 32 | tf_op jit(solution)/shard_map/psum | solution.py:230
  454.7 73.6 %psum.30 = f32[2,1,1]{0,2,1:T(1,128)S(1)} all-reduce(f32[2,1,1]{0,2,1:T(1,128)S(1)} %bitcast.451), channel_id=1, replica_groups=mesh['gx'=8,'gy'=32] {'gx','gy'}, use_global_device_ids=true, to_apply=%region_20.21 | all-reduce | flops 2 | bytes 16 | tf_op jit(solution)/shard_map/psum | solution.py:230
  540.0 2.5 collective-permute-done.15
  543.3 77.1 %psum.31 = f32[2,1,1]{0,2,1:T(1,128)S(1)} all-reduce(f32[2,1,1]{0,2,1:T(1,128)S(1)} %bitcast.450), channel_id=1, replica_groups=mesh['gx'=8,'gy'=32] {'gx','gy'}, use_global_device_ids=true, to_apply=%region_22.23 | all-reduce | flops 2 | bytes 16 | tf_op jit(solution)/shard_map/psum | solution.py:244
  (551 shorter events, 199.0 us)
Async XLA Ops:
  3.7 20.6 %collective-permute-start = (f32[3,4,64,32]{3,2,1,0:T(8,128)}, f32[3,4,64,32]{3,2,1,0:T(8,128)}, u32[]{:S(2)}, u32[]{:S(2)}) collective-permute-start(f32[3,4,64,32]{3,2,1,0:T(8,128)} %get-tuple-element.370), channel_id=1, source_target_pairs={{0,32},{32,64},{64,96},{96,128},{128,160},{160,192},{192,224},{224... | collective-permute-start | bytes 294920 | tf_op jit(solution)/shard_map/ppermute | solution.py:27
  6.1 19.5 %collective-permute-start.1 = (f32[3,4,64,32]{3,2,1,0:T(8,128)}, f32[3,4,64,32]{3,2,1,0:T(8,128)S(1)}, u32[]{:S(2)}, u32[]{:S(2)}) collective-permute-start(f32[3,4,64,32]{3,2,1,0:T(8,128)} %get-tuple-element.369), channel_id=1, source_target_pairs={{32,0},{64,32},{96,64},{128,96},{160,128},{192,160},{224,192},{0,2... | collective-permute-start | bytes 294920 | tf_op jit(solution)/shard_map/ppermute | solution.py:29
  10.1 20.1 %copy-start.18 = (f32[3]{0:T(128)}, f32[3]{0:T(128)S(1)}, u32[]{:S(2)}) copy-start(f32[3]{0:T(128)S(1)} %compare_convert_fusion) | copy-start | bytes 40
  10.1 8.1 %collective-permute-start.4 = (f32[2,2,3]{2,0,1:T(2,128)S(1)}, f32[2,2,3]{2,0,1:T(2,128)S(1)}, u32[]{:S(2)}, u32[]{:S(2)}) collective-permute-start(f32[2,2,3]{2,0,1:T(2,128)S(1)} %broadcast_in_dim.227), channel_id=1, source_target_pairs={{0,224},{32,0},{64,32},{96,64},{128,96},{160,128},{192,160},{224,1... | collective-permute-start | bytes 152 | tf_op jit(solution)/shard_map/ppermute | solution.py:17
  19.3 4.3 collective-permute-start.5
  25.4 4.9 copy-start.19
  27.6 7.9 %collective-permute-start.3 = (f32[3,40,4,32]{3,2,1,0:T(4,128)S(1)}, f32[3,40,4,32]{3,2,1,0:T(4,128)S(1)}, u32[]{:S(2)}, u32[]{:S(2)}) collective-permute-start(f32[3,40,4,32]{3,2,1,0:T(4,128)S(1)} %get-tuple-element.368), channel_id=1, source_target_pairs={{1,0},{2,1},{3,2},{4,3},{5,4},{6,5},{7,6},{8,7},{9,8},{10,9},{11,1... | collective-permute-start | bytes 184328 | tf_op jit(solution)/shard_map/ppermute | solution.py:29
  30.2 7.4 %collective-permute-start.2 = (f32[3,40,4,32]{3,2,1,0:T(4,128)S(1)}, f32[3,40,4,32]{3,2,1,0:T(4,128)S(1)}, u32[]{:S(2)}, u32[]{:S(2)}) collective-permute-start(f32[3,40,4,32]{3,2,1,0:T(4,128)S(1)} %get-tuple-element.367), channel_id=1, source_target_pairs={{0,1},{1,2},{2,3},{3,4},{4,5},{5,6},{6,7},{7,8},{8,9},{9,10},{10,1... | collective-permute-start | bytes 184328 | tf_op jit(solution)/shard_map/ppermute | solution.py:27
  39.7 4.5 copy-start.20
  66.1 3.0 copy-start.3
  125.3 4.6 copy-start.9
  125.3 4.6 copy-start.11
  185.8 2.6 copy-start.16
  186.3 3.2 copy-start.21
  186.3 2.6 copy-start.14
  211.6 3.0 copy-start.3
  270.5 4.6 copy-start.9
  270.5 4.6 copy-start.11
  331.8 3.2 copy-start.21
  331.8 2.6 copy-start.14
  344.8 7.3 %collective-permute-start.6 = (f32[2,2,3]{2,1,0:T(2,128)S(1)}, f32[2,2,3]{2,1,0:T(2,128)S(1)}, u32[]{:S(2)}, u32[]{:S(2)}) collective-permute-start(f32[2,2,3]{2,1,0:T(2,128)S(1)} %pad_maximum_fusion.19), channel_id=1, source_target_pairs={{0,1},{1,2},{2,3},{3,4},{4,5},{5,6},{6,7},{7,8},{8,9},{9,10},{10,1... | collective-permute-start | bytes 152 | tf_op jit(solution)/shard_map/ppermute | solution.py:17
  352.2 4.6 collective-permute-start.7
  357.6 2.4 collective-permute-start.8
  360.1 8.2 %collective-permute-start.9 = (f32[2,2,3]{2,1,0:T(2,128)S(1)}, f32[2,2,3]{2,1,0:T(2,128)S(1)}, u32[]{:S(2)}, u32[]{:S(2)}) collective-permute-start(f32[2,2,3]{2,1,0:T(2,128)S(1)} %pad_maximum_fusion.20), channel_id=1, source_target_pairs={{0,31},{1,0},{2,1},{3,2},{4,3},{5,4},{6,5},{7,6},{8,7},{9,8},{10,9... | collective-permute-start | bytes 152 | tf_op jit(solution)/shard_map/ppermute | solution.py:17
  370.2 1.2 collective-permute-start.10
  371.5 4.2 collective-permute-start.11
  528.5 2.7 collective-permute-start.12
  531.2 3.9 collective-permute-start.13
  537.0 1.2 collective-permute-start.14
  538.3 4.2 collective-permute-start.15
  621.2 2.7 collective-permute-start.16
  623.9 3.7 collective-permute-start.17
  (25 other events, 37.6 us)
where the time goes:
time: 646 us; the launch traced here: 635 us
  blocking collectives  229 us (35%)
  local copies, waits for them, and re-layouts  188 us (29%)
  other arithmetic  118 us (18%)
  waiting for transfers between devices  34.7 us (5%)
  starting transfers between devices  28.8 us (4%)
  matrix products  20.8 us (3%)
  loops' own time  14.6 us (2%)
    psum x2, blocking collectives, squares(): lax.psum(jnp.sum(residual * residual, axis=(1, 2), keepdims=True), ('gx',...  152 us
    psum x1, blocking collectives, spread_solve(): lax.psum(jnp.sum(direction * image, axis=(1, 2), keepdims=True), ('gx', '...  77.1 us
    reshape x2, local copies, waits for them, and re-layouts, coarsen(): grouped = block.reshape(comps, rows // 2, 2, width // 2, 2, depth // 2, 2)  52.5 us
    reduce_sum x2, other arithmetic, coarsen(): return 0.125 * jnp.sum(grouped, axis=(2, 4, 6))  39.3 us
    ppermute x14, waiting for transfers between devices, shifted(): lax.ppermute(shard, axis, [(i, (i + by) % count) for i in range(count)])  34.7 us
    ppermute x14, starting transfers between devices, shifted(): lax.ppermute(shard, axis, [(i, (i + by) % count) for i in range(count)])  19.8 us
    reshape x4, local copies, waits for them, and re-layouts, solve_column(): solution.reshape(8, count, depth, rows, width)  15.7 us
    slice x4, local copies, waits for them, and re-layouts, solve_column(): solution.reshape(8, count, depth, rows, width)  15 us
  transfers between devices with their start and end apart: 18, of which 14 were waited for; matrix products, arithmetic and copies ran while one was open for 2% of the time, Pallas kernels for 0%

commit v1 on v0

v1 whole, which is shorter than its diff:
```python
import functools

import jax
import jax.numpy as jnp
import numpy as np
from jax import lax
from jax.experimental import pallas as pl
from jax.experimental.pallas import tpu as pltpu
from jax.sharding import PartitionSpec as P

EL = 32
ELZ = 16
MX = 4
MZ = 2
LANES = 128
GROUP = 40
MESH = pl.DeviceIdType.MESH
F32 = jnp.float32
VLIMIT = 60 * 1024 * 1024


class Level:
    def __init__(self, nk, nx, zw, edge, edge_depth, margin, margin_depth, spacing):
        self.nk = nk
        self.nx = nx
        self.nxr = -(-nx // 8) * 8
        self.zw = zw
        self.nseg = GROUP // zw
        self.edge = edge
        self.edge_depth = edge_depth
        self.margin = margin
        self.margin_depth = margin_depth
        self.spacing = spacing


FINE = Level(13, 40, 20, EL, ELZ, MX, MZ, 1.0)
TWIN = Level(7, 20, 10, EL // 2, ELZ // 2, MX // 2, MZ // 2, 2.0)


def stencil_masks():
    masks = np.zeros((10, 8, LANES), np.float32)

    def put(e, a, b, q):
        s = (b - a) % 8
        if s > 4:
            a, s = b, 8 - s
        masks[e * 5 + s, a, q] += 1.0

    q = 0
    for a in range(4):
        for b in range(a, 4):
            put(0, 2 * a + 1, 2 * b + 1, q)
            put(1, 2 * a, 2 * b, q)
            q += 1
    for a in range(4):
        for b in range(4):
            put(0, 2 * a + 1, 2 * b, q)
        q += 1
    return masks


def coarsen_matrix():
    matrix = np.zeros((LANES, LANES), np.float32)
    for h in range(4):
        for e in range(2):
            for zz in range(10):
                for part in range(2):
                    z = min(max(e * ELZ - MZ + 2 * zz + part, 0), 31)
                    matrix[h * 32 + z, (h // 2) * 20 + e * 10 + zz] += 0.125
    return matrix


def lane_iota(rows):
    return lax.broadcasted_iota(jnp.int32, (rows, LANES), 1)


def groups(lane):
    return (lane >= 40).astype(jnp.int32) + (lane >= 80).astype(jnp.int32) + (lane >= 120).astype(jnp.int32)


def split_lane(level, lane):
    chunk = groups(lane)
    inner = lane - GROUP * chunk
    seg = jnp.zeros_like(lane)
    for s in range(1, level.nseg):
        seg = seg + (inner >= s * level.zw).astype(jnp.int32)
    return chunk, seg, inner - level.zw * seg


def harmonic(first, second, spacing):
    return spacing * 2.0 * first * second / (first + second)


def halo_kernel(perm, west, east, hx, hy, hc, send, recv):
    i = lax.axis_index("gx")
    j = lax.axis_index("gy")
    ni = lax.axis_size("gx")
    nj = lax.axis_size("gy")
    up, down = lax.rem(i + 1, ni), lax.rem(i + ni - 1, ni)
    right, left = lax.rem(j + 1, nj), lax.rem(j + nj - 1, nj)
    width = perm.shape[2]
    low, high = pl.ds(0, LANES), pl.ds(width - LANES, LANES)
    plans = [
        (east, hx.at[0], (up, j)),
        (west, hx.at[1], (down, j)),
        (perm.at[:, :, high], hy.at[0], (i, right)),
        (perm.at[:, :, low], hy.at[1], (i, left)),
        (east.at[:, :, high], hc.at[0], (up, right)),
        (east.at[:, :, low], hc.at[1], (up, left)),
        (west.at[:, :, high], hc.at[2], (down, right)),
        (west.at[:, :, low], hc.at[3], (down, left)),
    ]
    barrier = pltpu.get_barrier_semaphore()
    for _, _, target in plans:
        pl.semaphore_signal(barrier, inc=1, device_id=target, device_id_type=MESH)
    pl.semaphore_wait(barrier, 8)
    copies = []
    for n, (src, dst, target) in enumerate(plans):
        copy = pltpu.make_async_remote_copy(
            src_ref=src, dst_ref=dst, send_sem=send.at[n], recv_sem=recv.at[n],
            device_id=target, device_id_type=MESH,
        )
        copy.start()
        copies.append(copy)
    for copy in copies:
        copy.wait()


def halo(perm):
    rows, width = perm.shape[1], perm.shape[2]
    west = perm[:, :MX]
    east = perm[:, rows - MX:]
    anywhere = pl.BlockSpec(memory_space=pl.ANY)
    return pl.pallas_call(
        halo_kernel,
        out_shape=(
            jax.ShapeDtypeStruct((2, 3, MX, width), F32),
            jax.ShapeDtypeStruct((2, 3, rows, LANES), F32),
            jax.ShapeDtypeStruct((4, 3, MX, LANES), F32),
        ),
        in_specs=[anywhere] * 3,
        out_specs=(anywhere,) * 3,
        scratch_shapes=[pltpu.SemaphoreType.DMA((8,)), pltpu.SemaphoreType.DMA((8,))],
        compiler_params=pltpu.CompilerParams(collective_id=0, has_side_effects=True),
    )(perm, west, east)


def assemble(own, hx, hy, hc, ext):
    rows = own.shape[1]

    def body(m, carry):
        for t in range(18):
            if t == 0:
                top, mid, low = hc[0, m], hy[0, m], hc[2, m]
            elif t == 17:
                top, mid, low = hc[1, m], hy[1, m], hc[3, m]
            else:
                lanes = pl.ds((t - 1) * LANES, LANES)
                top, mid, low = hx[0, m, :, lanes], own[m, :, lanes], hx[1, m, :, lanes]
            ext[m, t, 0:MX, :] = top
            ext[m, t, MX:MX + rows, :] = mid
            ext[m, t, MX + rows:2 * MX + rows, :] = low
            ext[m, t, 2 * MX + rows:, :] = jnp.ones((8, LANES), F32)
        return carry

    lax.fori_loop(0, 3, body, 0)


def pack_fine(ext, packed, column):
    lane = lane_iota(GROUP)
    chunk, _, _ = split_lane(FINE, lane)
    inner = lane - GROUP * chunk

    def body(m, carry):
        for k in range(FINE.nk + 1):
            lines = []
            for c in range(3):
                y = FINE.nk * c + k
                tile = ext[m, column * 8 + y // 4, 0:40, :]
                shift = (c * GROUP - (y % 4) * 32) % LANES
                lines.append(pltpu.roll(tile, shift, 1) if shift else tile)
            q = jnp.where(chunk == 0, lines[0], jnp.where(chunk == 1, lines[1], lines[2]))
            out = jnp.where(inner == 0, q, pltpu.roll(q, 1, 1))
            out = jnp.where(inner > 1, pltpu.roll(q, 2, 1), out)
            out = jnp.where(inner > 19, pltpu.roll(q, 6, 1), out)
            out = jnp.where(inner > 37, pltpu.roll(q, 7, 1), out)
            out = jnp.where(inner > 38, pltpu.roll(q, 8, 1), out)
            packed[m, k, 0:40, :] = jnp.where(chunk < 3, out, 1.0)
            packed[m, k, 40:48, :] = jnp.ones((8, LANES), F32)
        return carry

    lax.fori_loop(0, 3, body, 0)


def pack_twin(ext, matrix, pairs, small, packed):
    lane = lane_iota(24)
    chunk = groups(lane)
    half = jnp.zeros_like(lane)
    for s in range(1, 7):
        half = half + (lane >= 20 * s).astype(jnp.int32)
    weights = matrix[...]

    def body(m, carry):
        for t in range(18):
            first = ext[m, t, pl.ds(0, 24, stride=2), :]
            second = ext[m, t, pl.ds(1, 24, stride=2), :]
            pairs[t * 24:(t + 1) * 24, :] = first + second
        value = pairs[...]
        high = value.astype(jnp.bfloat16)
        rest = value - high.astype(F32)
        mid = rest.astype(jnp.bfloat16)
        low = (rest - mid.astype(F32)).astype(jnp.bfloat16)
        small[...] = (
            jnp.dot(high, weights, preferred_element_type=F32)
            + jnp.dot(mid, weights, preferred_element_type=F32)
            + jnp.dot(low, weights, preferred_element_type=F32)
        )
        for k in range(TWIN.nk + 1):
            out = jnp.ones((24, LANES), F32)
            for c in range(3):
                y = min(TWIN.nk * c + k, TWIN.nx - 1)
                for col in range(2):
                    base = (col * 8 + y // 2) * 24
                    line = small[base:base + 24, :]
                    shift = (c * GROUP + col * 20 - (y % 2) * 20) % LANES
                    line = pltpu.roll(line, shift, 1) if shift else line
                    out = jnp.where(half == 2 * c + col, line, out)
            packed[m, k, 0:24, :] = out
            packed[m, k, 24:32, :] = jnp.ones((8, LANES), F32)
        return carry

    lax.fori_loop(0, 3, body, 0)


def face_arrays(level, packed, wt):
    nk, nx, nxr = level.nk, level.nx, level.nxr
    lane = lane_iota(nxr)
    chunk, seg, z = split_lane(level, lane)
    row = lax.broadcasted_iota(jnp.int32, (nxr, LANES), 0)
    ml, mz = level.margin, level.margin_depth
    inside_xz = (row > 0) & (row < nx - 1) & (z > 0) & (z < level.zw - 1) & (chunk < 3)
    el_x = (row >= ml) & (row < ml + level.edge)
    el_z = (z >= mz) & (z < mz + level.edge_depth) & (chunk < 3)
    el_xf = (row >= ml) & (row < ml + level.edge - 1)
    el_zf = (z >= mz) & (z < mz + level.edge_depth - 1) & (chunk < 3)

    def body(k, carry):
        y = chunk * nk + k
        inside = inside_xz & (y > 0) & (y < nx - 1)
        el_y = (y >= ml) & (y < ml + level.edge)
        el_yf = (y >= ml) & (y < ml + level.edge - 1)
        tx = harmonic(packed[0, k, 0:nxr, :], packed[0, k, 1:nxr + 1, :], level.spacing)
        ty = harmonic(packed[1, k, 0:nxr, :], packed[1, k + 1, 0:nxr, :], level.spacing)
        kz = packed[2, k, 0:nxr, :]
        tz = harmonic(kz, pltpu.roll(kz, LANES - 1, 1), level.spacing)
        wt[0, k] = tx
        wt[1, k] = ty
        wt[2, k] = tz
        wt[3, k] = jnp.where(inside, tx - pltpu.roll(tx, 1, 0), 0.0)
        wt[5, k] = jnp.where(inside, tz - pltpu.roll(tz, 1, 1), 0.0)
        wt[6, k] = jnp.where(el_xf & el_y & el_z, tx, 0.0)
        wt[7, k] = jnp.where(el_x & el_yf & el_z, ty, 0.0)
        wt[8, k] = jnp.where(el_x & el_y & el_zf, tz, 0.0)
        return carry

    lax.fori_loop(0, nk, body, 0)

    def inside_at(k):
        y = chunk * nk + k
        return inside_xz & (y > 0) & (y < nx - 1)

    wt[4, 0] = jnp.where(inside_at(0), wt[1, 0] - pltpu.roll(wt[1, nk - 1], GROUP, 1), 0.0)

    def second(k, carry):
        wt[4, k] = jnp.where(inside_at(k), wt[1, k] - wt[1, k - 1], 0.0)
        return carry

    lax.fori_loop(1, nk, second, 0)


def basis_solve(level, wt, cst, r0, r1, r2, w, store_phi):
    nk, nx = level.nk, level.nx
    lane = lane_iota(8)
    chunk, seg, z = split_lane(level, lane)
    sub = lax.broadcasted_iota(jnp.int32, (8, LANES), 0)
    ax, ay, az = sub >= 4, ((sub >> 1) & 1) == 1, (sub & 1) == 1

    def ramp(flag, place, length):
        return jnp.where(flag, place / length, 1.0 - place / length)

    fz = ramp(az, z.astype(F32) - level.margin_depth + 0.5, level.edge_depth)
    sx = jnp.where(ax, 1.0 / level.edge, -1.0 / level.edge)
    sy = jnp.where(ay, 1.0 / level.edge, -1.0 / level.edge)
    sz = jnp.where(az, 1.0 / level.edge_depth, -1.0 / level.edge_depth)
    cst[4, 0] = sy * fz
    cst[4, 1] = sx
    for k in range(nk):
        fy = ramp(ay, (chunk * nk + k).astype(F32) - level.margin + 0.5, level.edge)
        cst[0, k] = sx * fy * fz
        cst[1, k] = sz * fy
        cst[2, k] = fy * fz

    cst[4, 2] = jnp.where(ax, (0.5 - level.margin) / level.edge, 1.0 - (0.5 - level.margin) / level.edge)

    def fx_at(x):
        return cst[4, 2] + cst[4, 1] * x.astype(F32)

    def mask_at(k):
        y = chunk * nk + k
        return (y > 0) & (y < nx - 1) & (z > 0) & (z < level.zw - 1) & (chunk < 3)

    cst[4, 3] = jnp.zeros((8, LANES), F32)
    zero = cst[4, 3]

    def row(n, k, x):
        return wt[n, k, pl.ds(x, 8, stride=0), :]

    def operate(base, x, u_new, u_prev, fx_prev):
        fx_new, image = [], []
        fy_last = row(base + 1, nk - 1, x) * (u_prev[nk - 1] - pltpu.roll(u_prev[0], LANES - GROUP, 1))
        fy_prev = pltpu.roll(fy_last, GROUP, 1)
        for k in range(nk):
            flux = row(base, k, x) * (u_prev[k] - u_new[k])
            fx_new.append(flux)
            out = flux - fx_prev[k]
            fy = fy_last if k == nk - 1 else row(base + 1, k, x) * (u_prev[k] - u_prev[k + 1])
            out = out + (fy - fy_prev)
            fy_prev = fy
            fz_flux = row(base + 2, k, x) * (u_prev[k] - pltpu.roll(u_prev[k], LANES - 1, 1))
            image.append(out + (fz_flux - pltpu.roll(fz_flux, 1, 1)))
        return fx_new, image

    def sweep(produce, keep_u, keep_w):
        def body(x, carry):
            u_prev, fx_prev, rr, rw = carry
            u_new = produce(x)
            if keep_u is not None:
                for k in range(nk):
                    keep_u[x, k] = u_new[k]
            fx_new, image = operate(0, x - 1, u_new, u_prev, fx_prev)
            for k in range(nk):
                if keep_w is not None:
                    keep_w[x - 1, k] = image[k]
                rr = rr + u_prev[k] * u_prev[k]
                rw = rw + u_prev[k] * image[k]
            return u_new, fx_new, rr, rw

        start = ([zero] * nk, [zero] * nk, zero, zero)
        _, _, rr, rw = lax.fori_loop(1, nx, body, start)
        return rr, rw

    def by_segment(acc):
        out = zero
        for s in range(level.nseg):
            total = jnp.sum(jnp.where(seg == s, acc, 0.0), axis=1, keepdims=True)
            out = jnp.where(seg == s, total, out)
        return out

    for k in range(nk):
        w[nx - 1, k] = zero

    def first(x):
        fx = fx_at(x)
        return [
            row(3, k, x) * cst[0, k] + fx * (row(4, k, x) * cst[4, 0] + row(5, k, x) * cst[1, k])
            for k in range(nk)
        ]

    rr, rw = sweep(first, r0, w)
    rr0, rw0 = by_segment(rr), by_segment(rw)
    alpha0 = rr0 / rw0
    for k in range(nk):
        cst[3, k] = jnp.where(mask_at(k), alpha0, 0.0)
    rr, rw = sweep(lambda x: [r0[x, k] - cst[3, k] * w[x, k] for k in range(nk)], r1, w)
    rr1, rw1 = by_segment(rr), by_segment(rw)
    beta0 = rr1 / rr0
    alpha1 = rr1 / (rw1 - beta0 / alpha0 * rr1)
    gamma = alpha1 * beta0 / alpha0
    for k in range(nk):
        cst[3, k] = jnp.where(mask_at(k), alpha1, 0.0)

    def third(x):
        return [
            r1[x, k] + gamma * (r1[x, k] - r0[x, k]) - cst[3, k] * w[x, k] for k in range(nk)
        ]

    rr, rw = sweep(third, r2, None)
    rr2, rw2 = by_segment(rr), by_segment(rw)
    beta1 = rr2 / rr1
    alpha2 = rr2 / (rw2 - beta1 / alpha1 * rr2)
    c2 = alpha2
    c1 = alpha1 + alpha2 * beta1
    c0 = alpha0 + c1 * beta0

    def basis(x):
        fx = fx_at(x)
        return [
            fx * cst[2, k] + (c0 * r0[x, k] + (c1 * r1[x, k] + c2 * r2[x, k])) for k in range(nk)
        ]

    low = level.margin
    high = level.margin + level.edge

    def body(x, carry):
        u_prev, fx_prev, acc = carry
        u_new = basis(x)
        fx_new, image = operate(6, x - 1, u_new, u_prev, fx_prev)
        acc = list(acc)
        for k in range(nk):
            store_phi(x - 1 - low, k, u_prev[k])
            for s in range(5):
                turned = pltpu.roll(image[k], 8 - s, 0) if s else image[k]
                acc[s] = acc[s] + u_prev[k] * turned
        return u_new, fx_new, tuple(acc)

    start = (basis(jnp.int32(low)), [zero] * nk, (zero,) * 5)
    _, _, acc = lax.fori_loop(low + 1, high + 1, body, start)
    return acc, seg


def stencil(level, acc, seg, masks, elements):
    out = jnp.zeros((8, LANES), F32)
    for e, s in enumerate(elements):
        for n in range(5):
            total = jnp.sum(jnp.where(seg == s, acc[n], 0.0), axis=1, keepdims=True)
            out = out + total * masks[e * 5 + n]
    return out


def local_kernel(own, hx, hy, hc, matrix, masks, phi_f, phi_t, line, ext, pairs, small, pk_f, pk_t,
                 wt_f, wt_t, cst_f, cst_t, f0, f1, f2, fw, g0, g1, g2, gw):
    assemble(own, hx, hy, hc, ext)
    pack_twin(ext, matrix, pairs, small, pk_t)
    face_arrays(TWIN, pk_t, wt_t)

    def store_twin(x, k, value):
        phi_t[x, k] = value

    acc, seg = basis_solve(TWIN, wt_t, cst_t, g0, g1, g2, gw, store_twin)
    parts = [stencil(TWIN, acc, seg, masks, (2 * col, 2 * col + 1)) for col in range(2)]
    total = pltpu.roll(parts[0], 32, 1) + pltpu.roll(parts[1], 48, 1)

    def body(col, total):
        pack_fine(ext, pk_f, col)
        face_arrays(FINE, pk_f, wt_f)

        def store_fine(x, k, value):
            phi_f[col, x, k] = value

        acc, seg = basis_solve(FINE, wt_f, cst_f, f0, f1, f2, fw, store_fine)
        part = stencil(FINE, acc, seg, masks, (0, 1))
        here = jnp.full((8, LANES), col, jnp.int32) == 0
        return total + jnp.where(here, part, pltpu.roll(part, 16, 1))

    total = lax.fori_loop(0, 2, body, total)
    line[...] = jnp.broadcast_to(jnp.sum(total, axis=0, keepdims=True), (8, LANES))


def local_solve(perm, hx, hy, hc):
    vmem = pl.BlockSpec(memory_space=pltpu.VMEM)

    def fields(level):
        return [pltpu.VMEM((level.nx, level.nk, 8, LANES), F32)] * 4

    def scratch(level):
        return (
            pltpu.VMEM((3, level.nk + 1, level.nxr + 8, LANES), F32),
            pltpu.VMEM((9, level.nk, level.nxr, LANES), F32),
            pltpu.VMEM((5, level.nk, 8, LANES), F32),
        )

    pk_f, wt_f, cst_f = scratch(FINE)
    pk_t, wt_t, cst_t = scratch(TWIN)
    return pl.pallas_call(
        local_kernel,
        out_shape=(
            jax.ShapeDtypeStruct((2, EL, FINE.nk, 8, LANES), F32),
            jax.ShapeDtypeStruct((EL // 2, TWIN.nk, 8, LANES), F32),
            jax.ShapeDtypeStruct((8, LANES), F32),
        ),
        in_specs=[vmem] * 6,
        out_specs=(vmem,) * 3,
        scratch_shapes=[
            pltpu.VMEM((3, 18, 48, LANES), F32),
            pltpu.VMEM((18 * 24, LANES), F32),
            pltpu.VMEM((18 * 24, LANES), F32),
            pk_f, pk_t, wt_f, wt_t, cst_f, cst_t,
        ] + fields(FINE) + fields(TWIN),
        compiler_params=pltpu.CompilerParams(vmem_limit_bytes=VLIMIT),
    )(
        perm, hx, hy, hc,
        jnp.asarray(coarsen_matrix(), jnp.bfloat16), jnp.asarray(stencil_masks()),
    )


def coarse_solve(quantity, lane):
    second = (lane & 63) >= 32
    place = lane & 31

    def next_q(x):
        same = pltpu.roll(x, LANES - 32, 1)
        inner = pltpu.roll(x, 31, 1)
        outer = pltpu.roll(x, 63, 1)
        return jnp.where(second, jnp.where(place < 31, inner, outer), same)

    def prev_q(x):
        same = pltpu.roll(x, 32, 1)
        inner = pltpu.roll(x, LANES - 31, 1)
        outer = pltpu.roll(x, LANES - 63, 1)
        return jnp.where(second, same, jnp.where(place > 0, inner, outer))

    def next_p(x):
        return pltpu.roll(x, 7, 0)

    def prev_p(x):
        return pltpu.roll(x, 1, 0)

    entry = {}
    n = 0
    for a in range(4):
        for b in range(a, 4):
            entry[a, b] = entry[b, a] = quantity(n)
            n += 1

    def corners(x):
        side = next_q(x)
        return [x, side, next_p(x), next_p(side)]

    def gather(parts):
        side = prev_q(parts[1] + prev_p(parts[3]))
        return parts[0] + side + prev_p(parts[2])

    def operate(x):
        values = corners(x)
        parts = []
        for a in range(4):
            terms = [entry[a, b] * values[b] for b in range(4)]
            parts.append((terms[0] + terms[1]) + (terms[2] + terms[3]))
        return gather(parts)

    upper = lane >= 64

    def total(x):
        column = jnp.sum(x, axis=0, keepdims=True)
        lo = jnp.sum(jnp.where(upper[:1], 0.0, column), axis=1, keepdims=True)
        hi = jnp.sum(jnp.where(upper[:1], column, 0.0), axis=1, keepdims=True)
        return jnp.where(upper, hi, lo)

    residual = -gather([quantity(10 + a) for a in range(4)])
    norm = total(residual * residual)
    image = operate(residual)
    alpha = norm / total(residual * image)
    update = alpha * residual
    after = residual - alpha * image
    norm_next = total(after * after)
    direction = after + norm_next / norm * residual
    image = operate(direction)
    alpha = norm_next / total(direction * image)
    update = update + alpha * direction
    return [value for value in corners(update)]


def coarse_kernel(line, nodes, rows, block, grid, send1, recv1, send2, recv2):
    i = lax.axis_index("gx")
    j = lax.axis_index("gy")
    ni = lax.axis_size("gx")
    nj = lax.axis_size("gy")
    barrier = pltpu.get_barrier_semaphore()

    def greet_y(d, carry):
        pl.semaphore_signal(barrier, inc=1, device_id=(i, lax.rem(j + d, nj)), device_id_type=MESH)
        return carry

    def greet_x(d, carry):
        pl.semaphore_signal(barrier, inc=1, device_id=(lax.rem(i + d, ni), j), device_id_type=MESH)
        return carry

    lax.fori_loop(1, nj, greet_y, 0)
    lax.fori_loop(1, ni, greet_x, 0)
    pl.semaphore_wait(barrier, ni + nj - 2)

    def copy_y(d):
        return pltpu.make_async_remote_copy(
            src_ref=line, dst_ref=rows.at[j], send_sem=send1.at[d], recv_sem=recv1.at[d],
            device_id=(i, lax.rem(j + d, nj)), device_id_type=MESH,
        )

    def copy_x(d):
        return pltpu.make_async_remote_copy(
            src_ref=block, dst_ref=grid.at[i], send_sem=send2.at[d], recv_sem=recv2.at[d],
            device_id=(lax.rem(i + d, ni), j), device_id_type=MESH,
        )

    def start_y(d, carry):
        copy_y(d).start()
        return carry

    def wait_y(d, carry):
        copy_y(d).wait()
        return carry

    def start_x(d, carry):
        copy_x(d).start()
        return carry

    def wait_x(d, carry):
        copy_x(d).wait()
        return carry

    lax.fori_loop(1, nj, start_y, 0)
    rows[j] = line[...]
    lax.fori_loop(1, nj, wait_y, 0)
    quarter = rows[:, 0, :]
    turned = jnp.transpose(jnp.concatenate([quarter] * 4, axis=0))
    lane16 = lane_iota(16)
    out = turned[48:64]
    for b in range(3):
        out = jnp.where((lane16 >= 32 * b) & (lane16 < 32 * b + 32), turned[16 * b:16 * b + 16], out)
    block[...] = out
    lax.fori_loop(1, ni, start_x, 0)
    grid[i] = out
    lax.fori_loop(1, ni, wait_x, 0)
    values = coarse_solve(lambda q: grid[:, q, :], lane_iota(8))
    for a in range(4):
        nodes[a] = values[a]


def coarse(line, ni, nj):
    vmem = pl.BlockSpec(memory_space=pltpu.VMEM)
    return pl.pallas_call(
        coarse_kernel,
        out_shape=jax.ShapeDtypeStruct((4, 8, LANES), F32),
        in_specs=[vmem],
        out_specs=vmem,
        scratch_shapes=[
            pltpu.VMEM((nj, 8, LANES), F32),
            pltpu.VMEM((16, LANES), F32),
            pltpu.VMEM((ni, 16, LANES), F32),
            pltpu.SemaphoreType.DMA((nj,)),
            pltpu.SemaphoreType.DMA((nj,)),
            pltpu.SemaphoreType.DMA((ni,)),
            pltpu.SemaphoreType.DMA((ni,)),
        ],
        compiler_params=pltpu.CompilerParams(collective_id=1, has_side_effects=True),
    )(line)


def fold_rows(values, sub):
    low = sub < 4
    step = [
        jnp.where(low, values[n], values[n + 4])
        + pltpu.roll(jnp.where(low, values[n + 4], values[n]), 4, 0)
        for n in range(4)
    ]
    for shift in (2, 1):
        keep = (sub & shift) == 0
        step = [
            jnp.where(
                keep,
                step[n] + pltpu.roll(step[n], 8 - shift, 0),
                step[n + shift] + pltpu.roll(step[n + shift], shift, 0),
            )
            for n in range(shift)
        ]
    return step[0]


def pressure_kernel(phi_f, phi_t, nodes, fine, twin, rows_f, rows_t):
    i = lax.axis_index("gx")
    j = lax.axis_index("gy")
    sub = lax.broadcasted_iota(jnp.int32, (8, LANES), 0)
    lane = lane_iota(8)
    corner, az = sub >> 1, (sub & 1) == 1

    def own_nodes(level, col):
        here = (sub == i) & (lane == level * 64 + col * 32 + j)
        out = jnp.zeros((8, LANES), F32)
        for a in range(4):
            value = jnp.where(here, nodes[a], 0.0)
            value = jnp.sum(jnp.sum(value, axis=0, keepdims=True), axis=1, keepdims=True)
            out = jnp.where(corner == a, value, out)
        return jnp.where(az, out, 1.0), jnp.where(az, 0.0, out)

    _, seg, _ = split_lane(FINE, lane)
    fine_weights = []
    for col in range(2):
        first, second = own_nodes(0, col)
        fine_weights.append(jnp.where(seg == 0, first, second))
    _, seg, _ = split_lane(TWIN, lane)
    twin_weights = jnp.zeros((8, LANES), F32)
    for col in range(2):
        first, second = own_nodes(1, col)
        twin_weights = jnp.where(seg == 2 * col, first, twin_weights)
        twin_weights = jnp.where(seg == 2 * col + 1, second, twin_weights)

    def fine_rows(k, carry):
        for col in range(2):
            for g in range(EL // 8):
                values = [phi_f[col, 8 * g + n, k] * fine_weights[col] for n in range(8)]
                rows_f[col, k, 8 * g:8 * g + 8, :] = fold_rows(values, sub)
        return carry

    lax.fori_loop(0, FINE.nk, fine_rows, 0)

    def twin_rows(k, carry):
        for g in range(EL // 16):
            values = [phi_t[8 * g + n, k] * twin_weights for n in range(8)]
            rows_t[k, 8 * g:8 * g + 8, :] = fold_rows(values, sub)
        return carry

    lax.fori_loop(0, TWIN.nk, twin_rows, 0)

    def turn(value, shift):
        return pltpu.roll(value, shift % LANES, 1) if shift % LANES else value

    wide = lane_iota(EL)
    for col in range(2):
        for t in range(8):
            out = None
            for h in range(4):
                y = 4 * t + h + MX
                c, k = y // FINE.nk, y % FINE.nk
                for e in range(2):
                    to = h * 32 + e * 16
                    piece = turn(rows_f[col, k], to - (c * GROUP + e * 20 + MZ))
                    out = piece if out is None else jnp.where(wide >= to, piece, out)
            fine[:, (col * 8 + t) * LANES:(col * 8 + t + 1) * LANES] = out
    wide = lane_iota(EL // 2)
    for t in range(4):
        out = None
        for h in range(8):
            col, y = (8 * t + h) // 16, (8 * t + h) % 16 + MX // 2
            c, k = y // TWIN.nk, y % TWIN.nk
            for e in range(2):
                to = h * 16 + e * 8
                piece = turn(rows_t[k], to - (c * GROUP + col * 20 + e * 10 + MZ // 2))
                out = piece if out is None else jnp.where(wide >= to, piece, out)
        twin[:, t * LANES:(t + 1) * LANES] = out


def pressures(phi_f, phi_t, nodes):
    vmem = pl.BlockSpec(memory_space=pltpu.VMEM)
    return pl.pallas_call(
        pressure_kernel,
        out_shape=(
            jax.ShapeDtypeStruct((EL, 2048), F32),
            jax.ShapeDtypeStruct((EL // 2, 512), F32),
        ),
        in_specs=[vmem] * 3,
        out_specs=(vmem, vmem),
        scratch_shapes=[
            pltpu.VMEM((2, FINE.nk, EL, LANES), F32),
            pltpu.VMEM((TWIN.nk, EL // 2, LANES), F32),
        ],
        compiler_params=pltpu.CompilerParams(vmem_limit_bytes=VLIMIT),
    )(phi_f, phi_t, nodes)


def solution(mesh):
    ni, nj = mesh.shape["gx"], mesh.shape["gy"]

    def shards(perm):
        hx, hy, hc = halo(perm)
        phi_f, phi_t, line = local_solve(perm, hx, hy, hc)
        nodes = coarse(line, ni, nj)
        return pressures(phi_f, phi_t, nodes)

    return jax.shard_map(
        shards,
        mesh=mesh,
        in_specs=(P(None, "gx", "gy"),),
        out_specs=(P("gx", "gy"), P("gx", "gy")),
        check_vma=False,
    )
```

time: 646 us -> 117 us (0.18); the launches traced: 635 us -> 117 us
  blocking collectives: 229 us -> 0 us
  local copies, waits for them, and re-layouts: 188 us -> 1.73 us
  other arithmetic: 118 us -> 0 us
  Pallas kernels: 0 us -> 115 us
  waiting for transfers between devices: 34.7 us -> 0 us
  starting transfers between devices: 28.8 us -> 0 us
  matrix products: 20.8 us -> 0 us
  loops' own time: 14.6 us -> 0 us
    psum x3 -> x0, blocking collectives: 229 us -> none  [the longest x2 152 us: squares(): lax.psum(jnp.sum(residual * residual, axis=(1, 2), keepdims=True), ('gx',...]
    pallas_call x0 -> x4, Pallas kernels: none -> 115 us  [the longest x1 78.7 us: local_solve(): pl.pallas_call(local_kernel, out_shape=(jax.ShapeDtypeStruct((2, EL, FINE...]
    reshape x21 -> x0, local copies, waits for them, and re-layouts: 81.5 us -> none  [the longest x2 52.5 us: coarsen(): grouped = block.reshape(comps, rows // 2, 2, width // 2, 2, depth // 2, 2)]
    reduce_sum x27 -> x0, other arithmetic: 57.1 us -> none  [the longest x2 39.3 us: coarsen(): return 0.125 * jnp.sum(grouped, axis=(2, 4, 6))]
    ppermute x18 -> x0, waiting for transfers between devices: 34.7 us -> none  [the longest x14 34.7 us: shifted(): lax.ppermute(shard, axis, [(i, (i + by) % count) for i in range(count)])]
    mul x83 -> x0, other arithmetic: 33 us -> none  [the longest x20 11.3 us: apply_operator(): flux = weight_cols * (field[..., :-1] - field[..., 1:])]
    slice x33 -> x1, local copies, waits for them, and re-layouts: 32 us -> 1.73 us  [halo(): east = perm[:, rows - MX:]]
    ppermute x18 -> x0, starting transfers between devices: 28.8 us -> none  [the longest x14 19.8 us: shifted(): lax.ppermute(shard, axis, [(i, (i + by) % count) for i in range(count)])]
  transfers between devices with their start and end apart: 18 -> 0, of which waited for: 14 -> 0; matrix products, arithmetic and copies ran while one was open for 2% -> 0% of each run, Pallas kernels for 0% -> 0%
where the time goes in v1:
time: 117 us
  Pallas kernels  115 us (98%)
  local copies, waits for them, and re-layouts  1.73 us (1%)
    pallas_call x1, Pallas kernels, local_solve(): pl.pallas_call(local_kernel, out_shape=(jax.ShapeDtypeStruct((2, EL, FINE...  78.7 us
    pallas_call x1, Pallas kernels, coarse(): pl.pallas_call(coarse_kernel, out_shape=jax.ShapeDtypeStruct((4, 8, LANES...  16.3 us
    pallas_call x1, Pallas kernels, halo(): pl.pallas_call(halo_kernel, out_shape=(jax.ShapeDtypeStruct((2, 3, MX, wi...  15.2 us
    pallas_call x1, Pallas kernels, pressures(): pl.pallas_call(pressure_kernel, out_shape=(jax.ShapeDtypeStruct((EL, 2048...  4.32 us

profile of v1, /device:TPU:1, one launch (start us, length us, event | category | flops | bytes accessed | tf_op | source)
XLA Modules:
  0.0 116.9 jit_solution(1378567695613691431)
XLA Ops:
  0.6 1.7 %fusion = (f32[3,4,2048]{2,1,0:T(4,128)}, f32[3,4,2048]{2,1,0:T(4,128)}) fusion(f32[3,32,2048]{2,1,0:T(8,128)} %own.1), kind=kLoop, calls=%fused_computation | loop fusion | bytes 393216 | tf_op jit(solution)/shard_map/slice | solution.py:132
  2.4 15.2 %shard_map.50 = (f32[2,3,4,2048]{3,2,1,0:T(4,128)}, f32[2,3,32,128]{3,2,1,0:T(8,128)}, f32[4,3,4,128]{3,2,1,0:T(4,128)}) custom-call(f32[3,32,2048]{2,1,0:T(8,128)} %own.1, f32[3,4,2048]{2,1,0:T(4,128)} %get-tuple-element.15.west, f32[3,4,2048]{2,1,0:T(4,128)} %get-tuple-element.14.east), custom_call_target="tpu_custom_call" | custom-call | tf_op jit(solution)/shard_map/pallas_call | solution.py:134
  17.5 78.7 %shard_map.51 = (f32[2,32,13,8,128]{4,3,2,1,0:T(8,128)}, f32[16,7,8,128]{3,2,1,0:T(8,128)}, f32[8,128]{1,0:T(8,128)}) custom-call(f32[3,32,2048]{2,1,0:T(8,128)} %own.1, f32[2,3,4,2048]{3,2,1,0:T(4,128)} %get-tuple-element.8.hx, f32[2,3,32,128]{3,2,1,0:T(8,128)} %get-tuple-element.9.hy, f32[4,3,4,128]{3,2,1,0:T(4,128)} %get-tuple-element.10.hc, ...), custom_call_target="tpu_custom_call" | custom-call | tf_op jit(solution)/shard_map/pallas_call | solution.py:474
  96.3 16.3 %shard_map.52.nodes = f32[4,8,128]{2,1,0:T(8,128)} custom-call(f32[8,128]{1,0:T(8,128)} %get-tuple-element.13.line), custom_call_target="tpu_custom_call" | custom-call | tf_op jit(solution)/shard_map/pallas_call | solution.py:630
  112.6 4.3 %shard_map.53 = (f32[32,2048]{1,0:T(8,128)}, f32[16,512]{1,0:T(8,128)}) custom-call(f32[2,32,13,8,128]{4,3,2,1,0:T(8,128)} %get-tuple-element.11.phi_f, f32[16,7,8,128]{3,2,1,0:T(8,128)} %get-tuple-element.12.phi_t, f32[4,8,128]{2,1,0:T(8,128)} %shard_map.52.nodes), custom_call_target="tpu_custom_call" | custom-call | tf_op jit(solution)/shard_map/pallas_call | solution.py:743

commit v2 on v1

--- a/solution.py
+++ b/solution.py
@@ -17,6 +17,8 @@
 MESH = pl.DeviceIdType.MESH
 F32 = jnp.float32
 VLIMIT = 60 * 1024 * 1024
+FINE_PLANES = (4, 4)
+TWIN_PLANES = (10, 8)
 
 
 class Level:
@@ -166,7 +168,7 @@
     lax.fori_loop(0, 3, body, 0)
 
 
-def pack_fine(ext, packed, column):
+def pack_fine(ext, packed, merged, column):
     lane = lane_iota(GROUP)
     chunk, _, _ = split_lane(FINE, lane)
     inner = lane - GROUP * chunk
@@ -177,19 +179,23 @@
             for c in range(3):
                 y = FINE.nk * c + k
                 tile = ext[m, column * 8 + y // 4, 0:40, :]
-                shift = (c * GROUP - (y % 4) * 32) % LANES
+                shift = (c * GROUP + MZ - (y % 4) * 32) % LANES
                 lines.append(pltpu.roll(tile, shift, 1) if shift else tile)
-            q = jnp.where(chunk == 0, lines[0], jnp.where(chunk == 1, lines[1], lines[2]))
-            out = jnp.where(inner == 0, q, pltpu.roll(q, 1, 1))
-            out = jnp.where(inner > 1, pltpu.roll(q, 2, 1), out)
-            out = jnp.where(inner > 19, pltpu.roll(q, 6, 1), out)
-            out = jnp.where(inner > 37, pltpu.roll(q, 7, 1), out)
-            out = jnp.where(inner > 38, pltpu.roll(q, 8, 1), out)
-            packed[m, k, 0:40, :] = jnp.where(chunk < 3, out, 1.0)
+            merged[m, k] = jnp.where(lane < GROUP, lines[0], jnp.where(lane < 2 * GROUP, lines[1], lines[2]))
+        return carry
+
+    lax.fori_loop(0, 3, body, 0)
+
+    def widen(m, carry):
+        for k in range(FINE.nk + 1):
+            q = merged[m, k]
+            out = jnp.where(inner < MZ, pltpu.roll(q, LANES - 1, 1), q)
+            out = jnp.where(inner > 19, pltpu.roll(q, 4, 1), out)
+            packed[m, k, 0:40, :] = jnp.where(inner > 37, pltpu.roll(q, 5, 1), out)
             packed[m, k, 40:48, :] = jnp.ones((8, LANES), F32)
         return carry
 
-    lax.fori_loop(0, 3, body, 0)
+    lax.fori_loop(0, 3, widen, 0)
 
 
 def pack_twin(ext, matrix, pairs, small, packed):
@@ -232,7 +238,7 @@
     lax.fori_loop(0, 3, body, 0)
 
 
-def face_arrays(level, packed, wt):
+def face_arrays(level, packed, wt, ym, turned):
     nk, nx, nxr = level.nk, level.nx, level.nxr
     lane = lane_iota(nxr)
     chunk, seg, z = split_lane(level, lane)
@@ -243,6 +249,19 @@
     el_z = (z >= mz) & (z < mz + level.edge_depth) & (chunk < 3)
     el_xf = (row >= ml) & (row < ml + level.edge - 1)
     el_zf = (z >= mz) & (z < mz + level.edge_depth - 1) & (chunk < 3)
+    first_edge = seg == 0
+    if level.nseg == 4:
+        first_edge = first_edge | (seg == 2)
+    first_edge = first_edge & (z == 0)
+    last_edge = jnp.logical_not((seg == 0) | (seg == 2)) & (z == level.zw - 2)
+
+    el_zb = (z > mz) & (z < mz + level.edge_depth) & (chunk < 3)
+    below_first = (z == 1) & ((seg == 0) | (seg == 2))
+    below_last = (z == level.zw - 1) & jnp.logical_not((seg == 0) | (seg == 2))
+    for k in range(nk):
+        kz = packed[2, k, 0:nxr, :]
+        turned[0, k] = pltpu.roll(kz, LANES - 1, 1)
+        turned[1, k] = pltpu.roll(kz, 1, 1)
 
     def body(k, carry):
         y = chunk * nk + k
@@ -252,33 +271,44 @@
         tx = harmonic(packed[0, k, 0:nxr, :], packed[0, k, 1:nxr + 1, :], level.spacing)
         ty = harmonic(packed[1, k, 0:nxr, :], packed[1, k + 1, 0:nxr, :], level.spacing)
         kz = packed[2, k, 0:nxr, :]
-        tz = harmonic(kz, pltpu.roll(kz, LANES - 1, 1), level.spacing)
+        kz_after, kz_before, kz_here = turned[0, k], turned[1, k], kz
+        if level is FINE:
+            kz_here = jnp.where(first_edge, kz_after, kz)
+            kz_after = jnp.where(last_edge, kz, kz_after)
+            kz_before = jnp.where(below_first, kz, kz_before)
+            kz = jnp.where(below_last, kz_before, kz)
+        tz = harmonic(kz_here, kz_after, level.spacing)
+        tz_below = harmonic(kz_before, kz, level.spacing)
         wt[0, k] = tx
         wt[1, k] = ty
         wt[2, k] = tz
-        wt[3, k] = jnp.where(inside, tx - pltpu.roll(tx, 1, 0), 0.0)
-        wt[5, k] = jnp.where(inside, tz - pltpu.roll(tz, 1, 1), 0.0)
-        wt[6, k] = jnp.where(el_xf & el_y & el_z, tx, 0.0)
-        wt[7, k] = jnp.where(el_x & el_yf & el_z, ty, 0.0)
-        wt[8, k] = jnp.where(el_x & el_y & el_zf, tz, 0.0)
+        wt[3, k] = tz_below
+        wt[4, k] = jnp.where(inside, tx - pltpu.roll(tx, 1, 0), 0.0)
+        wt[6, k] = jnp.where(inside, tz - tz_below, 0.0)
+        wt[7, k] = jnp.where(el_xf & el_y & el_z, tx, 0.0)
+        wt[8, k] = jnp.where(el_x & el_yf & el_z, ty, 0.0)
+        wt[9, k] = jnp.where(el_x & el_y & el_zf, tz, 0.0)
+        wt[10, k] = jnp.where(el_x & el_y & el_zb, tz_below, 0.0)
         return carry
 
     lax.fori_loop(0, nk, body, 0)
+    ym[0] = pltpu.roll(wt[1, nk - 1], GROUP, 1)
+    ym[1] = pltpu.roll(wt[8, nk - 1], GROUP, 1)
 
     def inside_at(k):
         y = chunk * nk + k
         return inside_xz & (y > 0) & (y < nx - 1)
 
-    wt[4, 0] = jnp.where(inside_at(0), wt[1, 0] - pltpu.roll(wt[1, nk - 1], GROUP, 1), 0.0)
+    wt[5, 0] = jnp.where(inside_at(0), wt[1, 0] - ym[0], 0.0)
 
     def second(k, carry):
-        wt[4, k] = jnp.where(inside_at(k), wt[1, k] - wt[1, k - 1], 0.0)
+        wt[5, k] = jnp.where(inside_at(k), wt[1, k] - wt[1, k - 1], 0.0)
         return carry
 
     lax.fori_loop(1, nk, second, 0)
 
 
-def basis_solve(level, wt, cst, r0, r1, r2, w, store_phi):
+def basis_solve(level, wt, ym, cst, r0, r1, r2, w, above, below, beside, phi, planes):
     nk, nx = level.nk, level.nx
     lane = lane_iota(8)
     chunk, seg, z = split_lane(level, lane)
@@ -315,64 +345,94 @@
     def row(n, k, x):
         return wt[n, k, pl.ds(x, 8, stride=0), :]
 
-    def operate(base, x, u_new, u_prev, fx_prev):
-        fx_new, image = [], []
-        fy_last = row(base + 1, nk - 1, x) * (u_prev[nk - 1] - pltpu.roll(u_prev[0], LANES - GROUP, 1))
-        fy_prev = pltpu.roll(fy_last, GROUP, 1)
-        for k in range(nk):
-            flux = row(base, k, x) * (u_prev[k] - u_new[k])
-            fx_new.append(flux)
-            out = flux - fx_prev[k]
-            fy = fy_last if k == nk - 1 else row(base + 1, k, x) * (u_prev[k] - u_prev[k + 1])
-            out = out + (fy - fy_prev)
-            fy_prev = fy
-            fz_flux = row(base + 2, k, x) * (u_prev[k] - pltpu.roll(u_prev[k], LANES - 1, 1))
-            image.append(out + (fz_flux - pltpu.roll(fz_flux, 1, 1)))
-        return fx_new, image
-
-    def sweep(produce, keep_u, keep_w):
-        def body(x, carry):
-            u_prev, fx_prev, rr, rw = carry
-            u_new = produce(x)
-            if keep_u is not None:
+    def pipeline(base, low, high, depth, produce, keep, keep_w, consume, state):
+        def apply(x0, after, fx_prev, state):
+            ahead = [keep[x0, k] for k in range(nk)]
+            for p in range(depth):
+                x = x0 + p
+                u = ahead
+                ahead = after if p == depth - 1 else [keep[x + 1, k] for k in range(nk)]
+                fy_prev = ym[base // 7, pl.ds(x, 8, stride=0), :] * (beside[x, 1] - u[0])
+                image, fx_new = [], []
                 for k in range(nk):
-                    keep_u[x, k] = u_new[k]
-            fx_new, image = operate(0, x - 1, u_new, u_prev, fx_prev)
+                    flux = row(base, k, x) * (u[k] - ahead[k])
+                    fx_new.append(flux)
+                    out = flux - fx_prev[k]
+                    side = u[k + 1] if k < nk - 1 else beside[x, 0]
+                    fy = row(base + 1, k, x) * (u[k] - side)
+                    out = out + (fy - fy_prev)
+                    fy_prev = fy
+                    out = out + row(base + 2, k, x) * (u[k] - above[x, k])
+                    image.append(out + row(base + 3, k, x) * (u[k] - below[x, k]))
+                fx_prev = fx_new
+                if keep_w is not None:
+                    for k in range(nk):
+                        keep_w[x, k] = image[k]
+                for k in range(nk):
+                    state = consume(state, u[k], image[k])
+            return fx_prev, state
+
+        def store(x0, block):
+            for p in range(depth):
+                u = block[p]
+                for k in range(nk):
+                    keep[x0 + p, k] = u[k]
+                    above[x0 + p, k] = pltpu.roll(u[k], LANES - 1, 1)
+                    below[x0 + p, k] = pltpu.roll(u[k], 1, 1)
+                beside[x0 + p, 0] = pltpu.roll(u[0], LANES - GROUP, 1)
+                beside[x0 + p, 1] = pltpu.roll(u[nk - 1], GROUP, 1)
+
+        def make(x0):
+            return [produce(x0 + p) for p in range(depth)]
+
+        start = jnp.int32(low)
+        block = make(start)
+        fx_prev = [zero] * nk
+        store(start, block)
+
+        def body(n, carry):
+            fx_prev, state = carry
+            x0 = low + n * depth
+            block = make(x0)
+            fx_prev, state = apply(x0 - depth, block[0], fx_prev, state)
+            store(x0, block)
+            return fx_prev, state
+
+        count = (high - low) // depth
+        fx_prev, state = lax.fori_loop(1, count, body, (fx_prev, state))
+        _, state = apply(jnp.int32(high - depth), [zero] * nk, fx_prev, state)
+        return state
+
+    def norms(state, u, image):
+        return state[0] + u * u, state[1] + u * image
+
+    def sweep(produce, keep, keep_w):
+        state = pipeline(0, 0, nx, planes[0], produce, keep, keep_w, norms, (zero, zero))
+        if keep_w is not None:
             for k in range(nk):
-                if keep_w is not None:
-                    keep_w[x - 1, k] = image[k]
-                rr = rr + u_prev[k] * u_prev[k]
-                rw = rw + u_prev[k] * image[k]
-            return u_new, fx_new, rr, rw
-
-        start = ([zero] * nk, [zero] * nk, zero, zero)
-        _, _, rr, rw = lax.fori_loop(1, nx, body, start)
-        return rr, rw
+                keep_w[0, k] = zero
+                keep_w[nx - 1, k] = zero
+        return by_segment(state[0]), by_segment(state[1])
 
     def by_segment(acc):
-        out = zero
-        for s in range(level.nseg):
+        out = jnp.sum(jnp.where(seg == 0, acc, 0.0), axis=1, keepdims=True)
+        for s in range(1, level.nseg):
             total = jnp.sum(jnp.where(seg == s, acc, 0.0), axis=1, keepdims=True)
             out = jnp.where(seg == s, total, out)
         return out
 
-    for k in range(nk):
-        w[nx - 1, k] = zero
-
     def first(x):
         fx = fx_at(x)
         return [
-            row(3, k, x) * cst[0, k] + fx * (row(4, k, x) * cst[4, 0] + row(5, k, x) * cst[1, k])
+            row(4, k, x) * cst[0, k] + fx * (row(5, k, x) * cst[4, 0] + row(6, k, x) * cst[1, k])
             for k in range(nk)
         ]
 
-    rr, rw = sweep(first, r0, w)
-    rr0, rw0 = by_segment(rr), by_segment(rw)
+    rr0, rw0 = sweep(first, r0, w)
     alpha0 = rr0 / rw0
     for k in range(nk):
         cst[3, k] = jnp.where(mask_at(k), alpha0, 0.0)
-    rr, rw = sweep(lambda x: [r0[x, k] - cst[3, k] * w[x, k] for k in range(nk)], r1, w)
-    rr1, rw1 = by_segment(rr), by_segment(rw)
+    rr1, rw1 = sweep(lambda x: [r0[x, k] - cst[3, k] * w[x, k] for k in range(nk)], r1, w)
     beta0 = rr1 / rr0
     alpha1 = rr1 / (rw1 - beta0 / alpha0 * rr1)
     gamma = alpha1 * beta0 / alpha0
@@ -384,13 +444,13 @@
             r1[x, k] + gamma * (r1[x, k] - r0[x, k]) - cst[3, k] * w[x, k] for k in range(nk)
         ]
 
-    rr, rw = sweep(third, r2, None)
-    rr2, rw2 = by_segment(rr), by_segment(rw)
+    rr2, rw2 = sweep(third, r2, None)
     beta1 = rr2 / rr1
     alpha2 = rr2 / (rw2 - beta1 / alpha1 * rr2)
     c2 = alpha2
     c1 = alpha1 + alpha2 * beta1
     c0 = alpha0 + c1 * beta0
+    low = level.margin
 
     def basis(x):
         fx = fx_at(x)
@@ -398,23 +458,12 @@
             fx * cst[2, k] + (c0 * r0[x, k] + (c1 * r1[x, k] + c2 * r2[x, k])) for k in range(nk)
         ]
 
-    low = level.margin
-    high = level.margin + level.edge
-
-    def body(x, carry):
-        u_prev, fx_prev, acc = carry
-        u_new = basis(x)
-        fx_new, image = operate(6, x - 1, u_new, u_prev, fx_prev)
-        acc = list(acc)
-        for k in range(nk):
-            store_phi(x - 1 - low, k, u_prev[k])
-            for s in range(5):
-                turned = pltpu.roll(image[k], 8 - s, 0) if s else image[k]
-                acc[s] = acc[s] + u_prev[k] * turned
-        return u_new, fx_new, tuple(acc)
-
-    start = (basis(jnp.int32(low)), [zero] * nk, (zero,) * 5)
-    _, _, acc = lax.fori_loop(low + 1, high + 1, body, start)
+    def diagonals(state, u, image):
+        return tuple(
+            state[s] + u * (pltpu.roll(image, 8 - s, 0) if s else image) for s in range(5)
+        )
+
+    acc = pipeline(7, low, low + level.edge, planes[1], basis, phi, None, diagonals, (zero,) * 5)
     return acc, seg
 
 
@@ -427,27 +476,38 @@
     return out
 
 
-def local_kernel(own, hx, hy, hc, matrix, masks, phi_f, phi_t, line, ext, pairs, small, pk_f, pk_t,
-                 wt_f, wt_t, cst_f, cst_t, f0, f1, f2, fw, g0, g1, g2, gw):
+class Shifted:
+    def __init__(self, ref, first, column=None):
+        self.ref = ref
+        self.first = first
+        self.column = column
+
+    def place(self, index):
+        x, k = index
+        return (x - self.first, k) if self.column is None else (self.column, x - self.first, k)
+
+    def __getitem__(self, index):
+        return self.ref[self.place(index)]
+
+    def __setitem__(self, index, value):
+        self.ref[self.place(index)] = value
+
+
+def local_kernel(own, hx, hy, hc, matrix, masks, phi_f, phi_t, line, ext, pairs, small, merged, *scratch):
+    pk_f, wt_f, ym_f, turned_f, cst_f, *fields_f = scratch[:12]
+    pk_t, wt_t, ym_t, turned_t, cst_t, *fields_t = scratch[12:]
     assemble(own, hx, hy, hc, ext)
     pack_twin(ext, matrix, pairs, small, pk_t)
-    face_arrays(TWIN, pk_t, wt_t)
-
-    def store_twin(x, k, value):
-        phi_t[x, k] = value
-
-    acc, seg = basis_solve(TWIN, wt_t, cst_t, g0, g1, g2, gw, store_twin)
+    face_arrays(TWIN, pk_t, wt_t, ym_t, turned_t)
+    acc, seg = basis_solve(TWIN, wt_t, ym_t, cst_t, *fields_t, Shifted(phi_t, TWIN.margin), TWIN_PLANES)
     parts = [stencil(TWIN, acc, seg, masks, (2 * col, 2 * col + 1)) for col in range(2)]
     total = pltpu.roll(parts[0], 32, 1) + pltpu.roll(parts[1], 48, 1)
 
     def body(col, total):
-        pack_fine(ext, pk_f, col)
-        face_arrays(FINE, pk_f, wt_f)
-
-        def store_fine(x, k, value):
-            phi_f[col, x, k] = value
-
-        acc, seg = basis_solve(FINE, wt_f, cst_f, f0, f1, f2, fw, store_fine)
+        pack_fine(ext, pk_f, merged, col)
+        face_arrays(FINE, pk_f, wt_f, ym_f, turned_f)
+        phi = Shifted(phi_f, FINE.margin, col)
+        acc, seg = basis_solve(FINE, wt_f, ym_f, cst_f, *fields_f, phi, FINE_PLANES)
         part = stencil(FINE, acc, seg, masks, (0, 1))
         here = jnp.full((8, LANES), col, jnp.int32) == 0
         return total + jnp.where(here, part, pltpu.roll(part, 16, 1))
@@ -459,18 +519,16 @@
 def local_solve(perm, hx, hy, hc):
     vmem = pl.BlockSpec(memory_space=pltpu.VMEM)
 
-    def fields(level):
-        return [pltpu.VMEM((level.nx, level.nk, 8, LANES), F32)] * 4
-
     def scratch(level):
-        return (
+        field = pltpu.VMEM((level.nx, level.nk, 8, LANES), F32)
+        return [
             pltpu.VMEM((3, level.nk + 1, level.nxr + 8, LANES), F32),
-            pltpu.VMEM((9, level.nk, level.nxr, LANES), F32),
+            pltpu.VMEM((11, level.nk, level.nxr, LANES), F32),
+            pltpu.VMEM((2, level.nxr, LANES), F32),
+            pltpu.VMEM((2, level.nk, level.nxr, LANES), F32),
             pltpu.VMEM((5, level.nk, 8, LANES), F32),
-        )
-
-    pk_f, wt_f, cst_f = scratch(FINE)
-    pk_t, wt_t, cst_t = scratch(TWIN)
+        ] + [field] * 6 + [pltpu.VMEM((level.nx, 2, 8, LANES), F32)]
+
     return pl.pallas_call(
         local_kernel,
         out_shape=(
@@ -484,8 +542,8 @@
             pltpu.VMEM((3, 18, 48, LANES), F32),
             pltpu.VMEM((18 * 24, LANES), F32),
             pltpu.VMEM((18 * 24, LANES), F32),
-            pk_f, pk_t, wt_f, wt_t, cst_f, cst_t,
-        ] + fields(FINE) + fields(TWIN),
+            pltpu.VMEM((3, FINE.nk + 1, GROUP, LANES), F32),
+        ] + scratch(FINE) + scratch(TWIN),
         compiler_params=pltpu.CompilerParams(vmem_limit_bytes=VLIMIT),
     )(
         perm, hx, hy, hc,

time: 117 us -> 75.7 us (0.65)
  Pallas kernels: 115 us -> 73.2 us
    pallas_call x1, Pallas kernels: 78.7 us -> 37.4 us  [local_solve(): pl.pallas_call(local_kernel, out_shape=(jax.ShapeDtypeStruct((2, EL, FINE...]
where the time goes in v2:
time: 75.7 us; the launch traced here: 75.6 us
  Pallas kernels  73.2 us (97%)
  local copies, waits for them, and re-layouts  1.73 us (2%)
    pallas_call x1, Pallas kernels, local_solve(): pl.pallas_call(local_kernel, out_shape=(jax.ShapeDtypeStruct((2, EL, FINE...  37.4 us
    pallas_call x1, Pallas kernels, coarse(): pl.pallas_call(coarse_kernel, out_shape=jax.ShapeDtypeStruct((4, 8, LANES...  16.3 us
    pallas_call x1, Pallas kernels, halo(): pl.pallas_call(halo_kernel, out_shape=(jax.ShapeDtypeStruct((2, 3, MX, wi...  15.2 us
    pallas_call x1, Pallas kernels, pressures(): pl.pallas_call(pressure_kernel, out_shape=(jax.ShapeDtypeStruct((EL, 2048...  4.32 us
    slice x1, local copies, waits for them, and re-layouts, halo(): east = perm[:, rows - MX:]  1.73 us

profile of v2, /device:TPU:1, one launch (start us, length us, event | category | flops | bytes accessed | tf_op | source)
XLA Modules:
  0.0 75.6 jit_solution(11832532369488248959)
XLA Ops:
  0.6 1.7 %fusion = (f32[3,4,2048]{2,1,0:T(4,128)}, f32[3,4,2048]{2,1,0:T(4,128)}) fusion(f32[3,32,2048]{2,1,0:T(8,128)} %own.1), kind=kLoop, calls=%fused_computation | loop fusion | bytes 393216 | tf_op jit(solution)/shard_map/slice | solution.py:134
  2.4 15.2 %shard_map.50 = (f32[2,3,4,2048]{3,2,1,0:T(4,128)}, f32[2,3,32,128]{3,2,1,0:T(8,128)}, f32[4,3,4,128]{3,2,1,0:T(4,128)}) custom-call(f32[3,32,2048]{2,1,0:T(8,128)} %own.1, f32[3,4,2048]{2,1,0:T(4,128)} %get-tuple-element.15.west, f32[3,4,2048]{2,1,0:T(4,128)} %get-tuple-element.14.east), custom_call_target="tpu_custom_call" | custom-call | tf_op jit(solution)/shard_map/pallas_call | solution.py:136
  17.5 37.4 %shard_map.51 = (f32[2,32,13,8,128]{4,3,2,1,0:T(8,128)}, f32[16,7,8,128]{3,2,1,0:T(8,128)}, f32[8,128]{1,0:T(8,128)}) custom-call(f32[3,32,2048]{2,1,0:T(8,128)} %own.1, f32[2,3,4,2048]{3,2,1,0:T(4,128)} %get-tuple-element.8.hx, f32[2,3,32,128]{3,2,1,0:T(8,128)} %get-tuple-element.9.hy, f32[4,3,4,128]{3,2,1,0:T(4,128)} %get-tuple-element.10.hc, ...), custom_call_target="tpu_custom_call" | custom-call | tf_op jit(solution)/shard_map/pallas_call | solution.py:532
  55.0 16.3 %shard_map.52.nodes = f32[4,8,128]{2,1,0:T(8,128)} custom-call(f32[8,128]{1,0:T(8,128)} %get-tuple-element.13.line), custom_call_target="tpu_custom_call" | custom-call | tf_op jit(solution)/shard_map/pallas_call | solution.py:688
  71.3 4.3 %shard_map.53 = (f32[32,2048]{1,0:T(8,128)}, f32[16,512]{1,0:T(8,128)}) custom-call(f32[2,32,13,8,128]{4,3,2,1,0:T(8,128)} %get-tuple-element.11.phi_f, f32[16,7,8,128]{3,2,1,0:T(8,128)} %get-tuple-element.12.phi_t, f32[4,8,128]{2,1,0:T(8,128)} %shard_map.52.nodes), custom_call_target="tpu_custom_call" | custom-call | tf_op jit(solution)/shard_map/pallas_call | solution.py:801

commit v3 on v2

--- a/solution.py
+++ b/solution.py
@@ -93,7 +93,7 @@
     return spacing * 2.0 * first * second / (first + second)
 
 
-def halo_kernel(perm, west, east, hx, hy, hc, send, recv):
+def halo_kernel(perm, hx, hy, hc, send, recv):
     i = lax.axis_index("gx")
     j = lax.axis_index("gy")
     ni = lax.axis_size("gx")
@@ -101,6 +101,7 @@
     up, down = lax.rem(i + 1, ni), lax.rem(i + ni - 1, ni)
     right, left = lax.rem(j + 1, nj), lax.rem(j + nj - 1, nj)
     width = perm.shape[2]
+    west, east = perm.at[:, pl.ds(0, MX)], perm.at[:, pl.ds(perm.shape[1] - MX, MX)]
     low, high = pl.ds(0, LANES), pl.ds(width - LANES, LANES)
     plans = [
         (east, hx.at[0], (up, j)),
@@ -130,8 +131,6 @@
 
 def halo(perm):
     rows, width = perm.shape[1], perm.shape[2]
-    west = perm[:, :MX]
-    east = perm[:, rows - MX:]
     anywhere = pl.BlockSpec(memory_space=pl.ANY)
     return pl.pallas_call(
         halo_kernel,
@@ -140,11 +139,11 @@
             jax.ShapeDtypeStruct((2, 3, rows, LANES), F32),
             jax.ShapeDtypeStruct((4, 3, MX, LANES), F32),
         ),
-        in_specs=[anywhere] * 3,
+        in_specs=[anywhere],
         out_specs=(anywhere,) * 3,
         scratch_shapes=[pltpu.SemaphoreType.DMA((8,)), pltpu.SemaphoreType.DMA((8,))],
         compiler_params=pltpu.CompilerParams(collective_id=0, has_side_effects=True),
-    )(perm, west, east)
+    )(perm)
 
 
 def assemble(own, hx, hy, hc, ext):
@@ -493,7 +492,7 @@
         self.ref[self.place(index)] = value
 
 
-def local_kernel(own, hx, hy, hc, matrix, masks, phi_f, phi_t, line, ext, pairs, small, merged, *scratch):
+def local_work(own, hx, hy, hc, matrix, masks, phi_f, phi_t, line, ext, pairs, small, merged, *scratch):
     pk_f, wt_f, ym_f, turned_f, cst_f, *fields_f = scratch[:12]
     pk_t, wt_t, ym_t, turned_t, cst_t, *fields_t = scratch[12:]
     assemble(own, hx, hy, hc, ext)
@@ -516,9 +515,7 @@
     line[...] = jnp.broadcast_to(jnp.sum(total, axis=0, keepdims=True), (8, LANES))
 
 
-def local_solve(perm, hx, hy, hc):
-    vmem = pl.BlockSpec(memory_space=pltpu.VMEM)
-
+def local_scratch():
     def scratch(level):
         field = pltpu.VMEM((level.nx, level.nk, 8, LANES), F32)
         return [
@@ -529,26 +526,12 @@
             pltpu.VMEM((5, level.nk, 8, LANES), F32),
         ] + [field] * 6 + [pltpu.VMEM((level.nx, 2, 8, LANES), F32)]
 
-    return pl.pallas_call(
-        local_kernel,
-        out_shape=(
-            jax.ShapeDtypeStruct((2, EL, FINE.nk, 8, LANES), F32),
-            jax.ShapeDtypeStruct((EL // 2, TWIN.nk, 8, LANES), F32),
-            jax.ShapeDtypeStruct((8, LANES), F32),
-        ),
-        in_specs=[vmem] * 6,
-        out_specs=(vmem,) * 3,
-        scratch_shapes=[
-            pltpu.VMEM((3, 18, 48, LANES), F32),
-            pltpu.VMEM((18 * 24, LANES), F32),
-            pltpu.VMEM((18 * 24, LANES), F32),
-            pltpu.VMEM((3, FINE.nk + 1, GROUP, LANES), F32),
-        ] + scratch(FINE) + scratch(TWIN),
-        compiler_params=pltpu.CompilerParams(vmem_limit_bytes=VLIMIT),
-    )(
-        perm, hx, hy, hc,
-        jnp.asarray(coarsen_matrix(), jnp.bfloat16), jnp.asarray(stencil_masks()),
-    )
+    return [
+        pltpu.VMEM((3, 18, 48, LANES), F32),
+        pltpu.VMEM((18 * 24, LANES), F32),
+        pltpu.VMEM((18 * 24, LANES), F32),
+        pltpu.VMEM((3, FINE.nk + 1, GROUP, LANES), F32),
+    ] + scratch(FINE) + scratch(TWIN)
 
 
 def coarse_solve(quantity, lane):
@@ -618,7 +601,7 @@
     return [value for value in corners(update)]
 
 
-def coarse_kernel(line, nodes, rows, block, grid, send1, recv1, send2, recv2):
+def greet_groups():
     i = lax.axis_index("gx")
     j = lax.axis_index("gy")
     ni = lax.axis_size("gx")
@@ -635,7 +618,14 @@
 
     lax.fori_loop(1, nj, greet_y, 0)
     lax.fori_loop(1, ni, greet_x, 0)
-    pl.semaphore_wait(barrier, ni + nj - 2)
+
+
+def coarse_work(line, rows, block, grid, send1, recv1, send2, recv2):
+    i = lax.axis_index("gx")
+    j = lax.axis_index("gy")
+    ni = lax.axis_size("gx")
+    nj = lax.axis_size("gy")
+    pl.semaphore_wait(pltpu.get_barrier_semaphore(), ni + nj - 2)
 
     def copy_y(d):
         return pltpu.make_async_remote_copy(
@@ -678,29 +668,7 @@
     lax.fori_loop(1, ni, start_x, 0)
     grid[i] = out
     lax.fori_loop(1, ni, wait_x, 0)
-    values = coarse_solve(lambda q: grid[:, q, :], lane_iota(8))
-    for a in range(4):
-        nodes[a] = values[a]
-
-
-def coarse(line, ni, nj):
-    vmem = pl.BlockSpec(memory_space=pltpu.VMEM)
-    return pl.pallas_call(
-        coarse_kernel,
-        out_shape=jax.ShapeDtypeStruct((4, 8, LANES), F32),
-        in_specs=[vmem],
-        out_specs=vmem,
-        scratch_shapes=[
-            pltpu.VMEM((nj, 8, LANES), F32),
-            pltpu.VMEM((16, LANES), F32),
-            pltpu.VMEM((ni, 16, LANES), F32),
-            pltpu.SemaphoreType.DMA((nj,)),
-            pltpu.SemaphoreType.DMA((nj,)),
-            pltpu.SemaphoreType.DMA((ni,)),
-            pltpu.SemaphoreType.DMA((ni,)),
-        ],
-        compiler_params=pltpu.CompilerParams(collective_id=1, has_side_effects=True),
-    )(line)
+    return coarse_solve(lambda q: grid[:, q, :], lane_iota(8))
 
 
 def fold_rows(values, sub):
@@ -723,7 +691,7 @@
     return step[0]
 
 
-def pressure_kernel(phi_f, phi_t, nodes, fine, twin, rows_f, rows_t):
+def pressure_work(phi_f, phi_t, nodes, fine, twin, rows_f, rows_t):
     i = lax.axis_index("gx")
     j = lax.axis_index("gy")
     sub = lax.broadcasted_iota(jnp.int32, (8, LANES), 0)
@@ -796,22 +764,45 @@
         twin[:, t * LANES:(t + 1) * LANES] = out
 
 
-def pressures(phi_f, phi_t, nodes):
+def solve_kernel(own, hx, hy, hc, matrix, masks, fine, twin, phi_f, phi_t, rows_f, rows_t, line, *scratch):
+    exchange, local = scratch[:7], scratch[7:]
+    greet_groups()
+    local_work(own, hx, hy, hc, matrix, masks, phi_f, phi_t, line, *local)
+    nodes = coarse_work(line, *exchange)
+    pressure_work(phi_f, phi_t, nodes, fine, twin, rows_f, rows_t)
+
+
+def solve(perm, hx, hy, hc, ni, nj):
     vmem = pl.BlockSpec(memory_space=pltpu.VMEM)
     return pl.pallas_call(
-        pressure_kernel,
+        solve_kernel,
         out_shape=(
             jax.ShapeDtypeStruct((EL, 2048), F32),
             jax.ShapeDtypeStruct((EL // 2, 512), F32),
         ),
-        in_specs=[vmem] * 3,
+        in_specs=[vmem] * 6,
         out_specs=(vmem, vmem),
         scratch_shapes=[
+            pltpu.VMEM((2, EL, FINE.nk, 8, LANES), F32),
+            pltpu.VMEM((EL // 2, TWIN.nk, 8, LANES), F32),
             pltpu.VMEM((2, FINE.nk, EL, LANES), F32),
             pltpu.VMEM((TWIN.nk, EL // 2, LANES), F32),
-        ],
-        compiler_params=pltpu.CompilerParams(vmem_limit_bytes=VLIMIT),
-    )(phi_f, phi_t, nodes)
+            pltpu.VMEM((8, LANES), F32),
+            pltpu.VMEM((nj, 8, LANES), F32),
+            pltpu.VMEM((16, LANES), F32),
+            pltpu.VMEM((ni, 16, LANES), F32),
+            pltpu.SemaphoreType.DMA((nj,)),
+            pltpu.SemaphoreType.DMA((nj,)),
+            pltpu.SemaphoreType.DMA((ni,)),
+            pltpu.SemaphoreType.DMA((ni,)),
+        ] + local_scratch(),
+        compiler_params=pltpu.CompilerParams(
+            collective_id=1, has_side_effects=True, vmem_limit_bytes=VLIMIT
+        ),
+    )(
+        perm, hx, hy, hc,
+        jnp.asarray(coarsen_matrix(), jnp.bfloat16), jnp.asarray(stencil_masks()),
+    )
 
 
 def solution(mesh):
@@ -819,9 +810,7 @@
 
     def shards(perm):
         hx, hy, hc = halo(perm)
-        phi_f, phi_t, line = local_solve(perm, hx, hy, hc)
-        nodes = coarse(line, ni, nj)
-        return pressures(phi_f, phi_t, nodes)
+        return solve(perm, hx, hy, hc, ni, nj)
 
     return jax.shard_map(
         shards,

time: 75.7 us -> 68.5 us (0.905)
  Pallas kernels: 73.2 us -> 65.4 us
    pallas_call x3 -> x1, Pallas kernels: 58 us -> 50.1 us  [solve(): pl.pallas_call(solve_kernel, out_shape=(jax.ShapeDtypeStruct((EL, 2048),...]
    unnamed x0 -> x4, local copies, waits for them, and re-layouts: none -> 2.29 us
    slice x1 -> x0, local copies, waits for them, and re-layouts: 1.73 us -> none  [halo(): east = perm[:, rows - MX:]]
where the time goes in v3:
time: 68.5 us; the launch traced here: 68.4 us
  Pallas kernels  65.4 us (95%)
  local copies, waits for them, and re-layouts  2.29 us (3%)
    pallas_call x1, Pallas kernels, solve(): pl.pallas_call(solve_kernel, out_shape=(jax.ShapeDtypeStruct((EL, 2048),...  50.1 us
    pallas_call x1, Pallas kernels, halo(): pl.pallas_call(halo_kernel, out_shape=(jax.ShapeDtypeStruct((2, 3, MX, wi...  15.4 us
    unnamed x4, local copies, waits for them, and re-layouts  2.29 us

profile of v3, /device:TPU:1, one launch (start us, length us, event | category | flops | bytes accessed | tf_op | source)
XLA Modules:
  0.0 68.4 jit_solution(10289426896817671354)
XLA Ops:
  0.6 15.4 %shard_map.50 = (f32[2,3,4,2048]{3,2,1,0:T(4,128)}, f32[2,3,32,128]{3,2,1,0:T(8,128)}, f32[4,3,4,128]{3,2,1,0:T(4,128)}) custom-call(f32[3,32,2048]{2,1,0:T(8,128)} %own.1), custom_call_target="tpu_custom_call" | custom-call | tf_op jit(solution)/shard_map/pallas_call | solution.py:135
  16.0 50.1 %shard_map.51 = (f32[32,2048]{1,0:T(8,128)}, f32[16,512]{1,0:T(8,128)}) custom-call(f32[3,32,2048]{2,1,0:T(8,128)} %own.1, f32[2,3,4,2048]{3,2,1,0:T(4,128)} %get-tuple-element.5.hx, f32[2,3,32,128]{3,2,1,0:T(8,128)} %get-tuple-element.6.hy, f32[4,3,4,128]{3,2,1,0:T(4,128)} %get-tuple-element.7.hc, bf16[128,128]{1,0:T(8,128)(2,1)} %constant.4.clone.matrix, ...), custom_call_target="tpu_custom_call" | custom-call | tf_op jit(solution)/shard_map/pallas_call | solution.py:777
  66.1 0.0 copy-start
  66.1 1.7 %copy.7 = f32[32,2048]{1,0:T(8,128)} copy(f32[32,2048]{1,0:T(8,128)} %get-tuple-element.10) | data formatting | bytes 524288
  67.8 0.0 copy-done
  67.8 0.6 copy.8
Async XLA Ops:
  66.1 1.7 %copy-start = (f32[16,512]{1,0:T(8,128)S(1)}, f32[16,512]{1,0:T(8,128)}, u32[]{:S(2)}) copy-start(f32[16,512]{1,0:T(8,128)} %get-tuple-element.11) | copy-start | bytes 98308

commit v4 on v3

--- a/solution.py
+++ b/solution.py
@@ -18,7 +18,7 @@
 F32 = jnp.float32
 VLIMIT = 60 * 1024 * 1024
 FINE_PLANES = (4, 4)
-TWIN_PLANES = (10, 8)
+TWIN_PLANES = (5, 8)
 
 
 class Level:
@@ -307,7 +307,9 @@
     lax.fori_loop(1, nk, second, 0)
 
 
-def basis_solve(level, wt, ym, cst, r0, r1, r2, w, above, below, beside, phi, planes):
+def basis_solve(level, wt, ym, cst, r0, r1, r2, w, w2, *rest):
+    *rings, phi, planes = rest
+    rings = rings[:4], rings[4:]
     nk, nx = level.nk, level.nx
     lane = lane_iota(8)
     chunk, seg, z = split_lane(level, lane)
@@ -345,61 +347,63 @@
         return wt[n, k, pl.ds(x, 8, stride=0), :]
 
     def pipeline(base, low, high, depth, produce, keep, keep_w, consume, state):
-        def apply(x0, after, fx_prev, state):
-            ahead = [keep[x0, k] for k in range(nk)]
+        def apply(ring, x0, after, fx_prev, state):
+            u_ring, above, below, beside = ring
+            ahead = [u_ring[0, k] for k in range(nk)]
             for p in range(depth):
                 x = x0 + p
                 u = ahead
-                ahead = after if p == depth - 1 else [keep[x + 1, k] for k in range(nk)]
-                fy_prev = ym[base // 7, pl.ds(x, 8, stride=0), :] * (beside[x, 1] - u[0])
+                ahead = after if p == depth - 1 else [u_ring[p + 1, k] for k in range(nk)]
+                fy_prev = ym[base // 7, pl.ds(x, 8, stride=0), :] * (beside[p, 1] - u[0])
                 image, fx_new = [], []
                 for k in range(nk):
                     flux = row(base, k, x) * (u[k] - ahead[k])
                     fx_new.append(flux)
                     out = flux - fx_prev[k]
-                    side = u[k + 1] if k < nk - 1 else beside[x, 0]
+                    side = u[k + 1] if k < nk - 1 else beside[p, 0]
                     fy = row(base + 1, k, x) * (u[k] - side)
                     out = out + (fy - fy_prev)
                     fy_prev = fy
-                    out = out + row(base + 2, k, x) * (u[k] - above[x, k])
-                    image.append(out + row(base + 3, k, x) * (u[k] - below[x, k]))
+                    out = out + row(base + 2, k, x) * (u[k] - above[p, k])
+                    image.append(out + row(base + 3, k, x) * (u[k] - below[p, k]))
+                    if keep_w is not None:
+                        keep_w[x, k] = image[k]
+                    state = consume(state, u[k], image[k])
                 fx_prev = fx_new
-                if keep_w is not None:
-                    for k in range(nk):
-                        keep_w[x, k] = image[k]
-                for k in range(nk):
-                    state = consume(state, u[k], image[k])
             return fx_prev, state
 
-        def store(x0, block):
+        def make(ring, x0):
+            u_ring, above, below, beside = ring
+            first = None
             for p in range(depth):
-                u = block[p]
+                u = produce(x0 + p)
+                first = u if first is None else first
                 for k in range(nk):
                     keep[x0 + p, k] = u[k]
-                    above[x0 + p, k] = pltpu.roll(u[k], LANES - 1, 1)
-                    below[x0 + p, k] = pltpu.roll(u[k], 1, 1)
-                beside[x0 + p, 0] = pltpu.roll(u[0], LANES - GROUP, 1)
-                beside[x0 + p, 1] = pltpu.roll(u[nk - 1], GROUP, 1)
-
-        def make(x0):
-            return [produce(x0 + p) for p in range(depth)]
-
-        start = jnp.int32(low)
-        block = make(start)
-        fx_prev = [zero] * nk
-        store(start, block)
+                    u_ring[p, k] = u[k]
+                    above[p, k] = pltpu.roll(u[k], LANES - 1, 1)
+                    below[p, k] = pltpu.roll(u[k], 1, 1)
+                beside[p, 0] = pltpu.roll(u[0], LANES - GROUP, 1)
+                beside[p, 1] = pltpu.roll(u[nk - 1], GROUP, 1)
+            return first
+
+        even, odd = rings
+        make(even, jnp.int32(low))
 
         def body(n, carry):
             fx_prev, state = carry
-            x0 = low + n * depth
-            block = make(x0)
-            fx_prev, state = apply(x0 - depth, block[0], fx_prev, state)
-            store(x0, block)
-            return fx_prev, state
-
-        count = (high - low) // depth
-        fx_prev, state = lax.fori_loop(1, count, body, (fx_prev, state))
-        _, state = apply(jnp.int32(high - depth), [zero] * nk, fx_prev, state)
+            x0 = low + n * (2 * depth)
+            after = make(odd, x0 + depth)
+            fx_prev, state = apply(even, x0, after, fx_prev, state)
+            after = make(even, x0 + 2 * depth)
+            return apply(odd, x0 + depth, after, fx_prev, state)
+
+        count = (high - low) // (2 * depth)
+        fx_prev, state = lax.fori_loop(0, count - 1, body, ([zero] * nk, state))
+        x0 = jnp.int32(high - 2 * depth)
+        after = make(odd, x0 + depth)
+        fx_prev, state = apply(even, x0, after, fx_prev, state)
+        _, state = apply(odd, x0 + depth, [zero] * nk, fx_prev, state)
         return state
 
     def norms(state, u, image):
@@ -431,7 +435,7 @@
     alpha0 = rr0 / rw0
     for k in range(nk):
         cst[3, k] = jnp.where(mask_at(k), alpha0, 0.0)
-    rr1, rw1 = sweep(lambda x: [r0[x, k] - cst[3, k] * w[x, k] for k in range(nk)], r1, w)
+    rr1, rw1 = sweep(lambda x: [r0[x, k] - cst[3, k] * w[x, k] for k in range(nk)], r1, w2)
     beta0 = rr1 / rr0
     alpha1 = rr1 / (rw1 - beta0 / alpha0 * rr1)
     gamma = alpha1 * beta0 / alpha0
@@ -440,7 +444,7 @@
 
     def third(x):
         return [
-            r1[x, k] + gamma * (r1[x, k] - r0[x, k]) - cst[3, k] * w[x, k] for k in range(nk)
+            r1[x, k] + gamma * (r1[x, k] - r0[x, k]) - cst[3, k] * w2[x, k] for k in range(nk)
         ]
 
     rr2, rw2 = sweep(third, r2, None)
@@ -493,8 +497,8 @@
 
 
 def local_work(own, hx, hy, hc, matrix, masks, phi_f, phi_t, line, ext, pairs, small, merged, *scratch):
-    pk_f, wt_f, ym_f, turned_f, cst_f, *fields_f = scratch[:12]
-    pk_t, wt_t, ym_t, turned_t, cst_t, *fields_t = scratch[12:]
+    pk_f, wt_f, ym_f, turned_f, cst_f, *fields_f = scratch[:18]
+    pk_t, wt_t, ym_t, turned_t, cst_t, *fields_t = scratch[18:]
     assemble(own, hx, hy, hc, ext)
     pack_twin(ext, matrix, pairs, small, pk_t)
     face_arrays(TWIN, pk_t, wt_t, ym_t, turned_t)
@@ -512,11 +516,11 @@
         return total + jnp.where(here, part, pltpu.roll(part, 16, 1))
 
     total = lax.fori_loop(0, 2, body, total)
-    line[...] = jnp.broadcast_to(jnp.sum(total, axis=0, keepdims=True), (8, LANES))
+    line[...] = jnp.sum(total, axis=0, keepdims=True)
 
 
 def local_scratch():
-    def scratch(level):
+    def scratch(level, depth):
         field = pltpu.VMEM((level.nx, level.nk, 8, LANES), F32)
         return [
             pltpu.VMEM((3, level.nk + 1, level.nxr + 8, LANES), F32),
@@ -524,14 +528,16 @@
             pltpu.VMEM((2, level.nxr, LANES), F32),
             pltpu.VMEM((2, level.nk, level.nxr, LANES), F32),
             pltpu.VMEM((5, level.nk, 8, LANES), F32),
-        ] + [field] * 6 + [pltpu.VMEM((level.nx, 2, 8, LANES), F32)]
+        ] + [field] * 5 + (
+            [pltpu.VMEM((depth, level.nk, 8, LANES), F32)] * 3 + [pltpu.VMEM((depth, 2, 8, LANES), F32)]
+        ) * 2
 
     return [
         pltpu.VMEM((3, 18, 48, LANES), F32),
         pltpu.VMEM((18 * 24, LANES), F32),
         pltpu.VMEM((18 * 24, LANES), F32),
         pltpu.VMEM((3, FINE.nk + 1, GROUP, LANES), F32),
-    ] + scratch(FINE) + scratch(TWIN)
+    ] + scratch(FINE, max(FINE_PLANES)) + scratch(TWIN, max(TWIN_PLANES))
 
 
 def coarse_solve(quantity, lane):
@@ -635,7 +641,7 @@
 
     def copy_x(d):
         return pltpu.make_async_remote_copy(
-            src_ref=block, dst_ref=grid.at[i], send_sem=send2.at[d], recv_sem=recv2.at[d],
+            src_ref=block, dst_ref=grid.at[pl.ds(pl.multiple_of(i * 16, 16), 16)], send_sem=send2.at[d], recv_sem=recv2.at[d],
             device_id=(lax.rem(i + d, ni), j), device_id_type=MESH,
         )
 
@@ -666,9 +672,9 @@
         out = jnp.where((lane16 >= 32 * b) & (lane16 < 32 * b + 32), turned[16 * b:16 * b + 16], out)
     block[...] = out
     lax.fori_loop(1, ni, start_x, 0)
-    grid[i] = out
+    grid[pl.ds(pl.multiple_of(i * 16, 16), 16), :] = out
     lax.fori_loop(1, ni, wait_x, 0)
-    return coarse_solve(lambda q: grid[:, q, :], lane_iota(8))
+    return coarse_solve(lambda q: grid[pl.ds(q, 8, stride=16), :], lane_iota(8))
 
 
 def fold_rows(values, sub):
@@ -787,10 +793,10 @@
             pltpu.VMEM((EL // 2, TWIN.nk, 8, LANES), F32),
             pltpu.VMEM((2, FINE.nk, EL, LANES), F32),
             pltpu.VMEM((TWIN.nk, EL // 2, LANES), F32),
-            pltpu.VMEM((8, LANES), F32),
-            pltpu.VMEM((nj, 8, LANES), F32),
+            pltpu.VMEM((1, LANES), F32),
+            pltpu.VMEM((nj, 1, LANES), F32),
             pltpu.VMEM((16, LANES), F32),
-            pltpu.VMEM((ni, 16, LANES), F32),
+            pltpu.VMEM((ni * 16, LANES), F32),
             pltpu.SemaphoreType.DMA((nj,)),
             pltpu.SemaphoreType.DMA((nj,)),
             pltpu.SemaphoreType.DMA((ni,)),

time: 68.5 us -> 63.7 us (0.930)
  Pallas kernels: 65.4 us -> 60.7 us
    pallas_call x1, Pallas kernels: 50.1 us -> 45.3 us  [solve(): pl.pallas_call(solve_kernel, out_shape=(jax.ShapeDtypeStruct((EL, 2048),...]
where the time goes in v4:
time: 63.7 us; the launch traced here: 63.6 us
  Pallas kernels  60.7 us (95%)
  local copies, waits for them, and re-layouts  2.29 us (4%)
  between operations  0.65 us (1%)
    pallas_call x1, Pallas kernels, solve(): pl.pallas_call(solve_kernel, out_shape=(jax.ShapeDtypeStruct((EL, 2048),...  45.3 us
    pallas_call x1, Pallas kernels, halo(): pl.pallas_call(halo_kernel, out_shape=(jax.ShapeDtypeStruct((2, 3, MX, wi...  15.4 us
    unnamed x4, local copies, waits for them, and re-layouts  2.29 us

profile of v4, /device:TPU:1, one launch (start us, length us, event | category | flops | bytes accessed | tf_op | source)
XLA Modules:
  0.0 63.6 jit_solution(3873098793753623916)
XLA Ops:
  0.6 15.4 %shard_map.50 = (f32[2,3,4,2048]{3,2,1,0:T(4,128)}, f32[2,3,32,128]{3,2,1,0:T(8,128)}, f32[4,3,4,128]{3,2,1,0:T(4,128)}) custom-call(f32[3,32,2048]{2,1,0:T(8,128)} %own.1), custom_call_target="tpu_custom_call" | custom-call | tf_op jit(solution)/shard_map/pallas_call | solution.py:135
  16.0 45.3 %shard_map.51 = (f32[32,2048]{1,0:T(8,128)}, f32[16,512]{1,0:T(8,128)}) custom-call(f32[3,32,2048]{2,1,0:T(8,128)} %own.1, f32[2,3,4,2048]{3,2,1,0:T(4,128)} %get-tuple-element.5.hx, f32[2,3,32,128]{3,2,1,0:T(8,128)} %get-tuple-element.6.hy, f32[4,3,4,128]{3,2,1,0:T(4,128)} %get-tuple-element.7.hc, bf16[128,128]{1,0:T(8,128)(2,1)} %constant.4.clone.matrix, ...), custom_call_target="tpu_custom_call" | custom-call | tf_op jit(solution)/shard_map/pallas_call | solution.py:783
  61.3 0.0 copy-start
  61.3 1.7 %copy.7 = f32[32,2048]{1,0:T(8,128)} copy(f32[32,2048]{1,0:T(8,128)} %get-tuple-element.10) | data formatting | bytes 524288
  63.0 0.0 copy-done
  63.0 0.6 copy.8
Async XLA Ops:
  61.3 1.7 %copy-start = (f32[16,512]{1,0:T(8,128)S(1)}, f32[16,512]{1,0:T(8,128)}, u32[]{:S(2)}) copy-start(f32[16,512]{1,0:T(8,128)} %get-tuple-element.11) | copy-start | bytes 98308

commit v5 on v4

--- a/solution.py
+++ b/solution.py
@@ -93,57 +93,36 @@
     return spacing * 2.0 * first * second / (first + second)
 
 
-def halo_kernel(perm, hx, hy, hc, send, recv):
+def halo_plans(perm, hx, hy, hc):
     i = lax.axis_index("gx")
     j = lax.axis_index("gy")
     ni = lax.axis_size("gx")
     nj = lax.axis_size("gy")
     up, down = lax.rem(i + 1, ni), lax.rem(i + ni - 1, ni)
     right, left = lax.rem(j + 1, nj), lax.rem(j + nj - 1, nj)
-    width = perm.shape[2]
-    west, east = perm.at[:, pl.ds(0, MX)], perm.at[:, pl.ds(perm.shape[1] - MX, MX)]
+    rows, width = perm.shape[1], perm.shape[2]
+    west, east = pl.ds(0, MX), pl.ds(rows - MX, MX)
     low, high = pl.ds(0, LANES), pl.ds(width - LANES, LANES)
-    plans = [
-        (east, hx.at[0], (up, j)),
-        (west, hx.at[1], (down, j)),
+    return [
+        (perm.at[:, east], hx.at[0], (up, j)),
+        (perm.at[:, west], hx.at[1], (down, j)),
         (perm.at[:, :, high], hy.at[0], (i, right)),
         (perm.at[:, :, low], hy.at[1], (i, left)),
-        (east.at[:, :, high], hc.at[0], (up, right)),
-        (east.at[:, :, low], hc.at[1], (up, left)),
-        (west.at[:, :, high], hc.at[2], (down, right)),
-        (west.at[:, :, low], hc.at[3], (down, left)),
+        (perm.at[:, east, high], hc.at[0], (up, right)),
+        (perm.at[:, east, low], hc.at[1], (up, left)),
+        (perm.at[:, west, high], hc.at[2], (down, right)),
+        (perm.at[:, west, low], hc.at[3], (down, left)),
     ]
-    barrier = pltpu.get_barrier_semaphore()
-    for _, _, target in plans:
-        pl.semaphore_signal(barrier, inc=1, device_id=target, device_id_type=MESH)
-    pl.semaphore_wait(barrier, 8)
-    copies = []
-    for n, (src, dst, target) in enumerate(plans):
-        copy = pltpu.make_async_remote_copy(
+
+
+def halo_copies(plans, send, recv):
+    return [
+        pltpu.make_async_remote_copy(
             src_ref=src, dst_ref=dst, send_sem=send.at[n], recv_sem=recv.at[n],
             device_id=target, device_id_type=MESH,
         )
-        copy.start()
-        copies.append(copy)
-    for copy in copies:
-        copy.wait()
-
-
-def halo(perm):
-    rows, width = perm.shape[1], perm.shape[2]
-    anywhere = pl.BlockSpec(memory_space=pl.ANY)
-    return pl.pallas_call(
-        halo_kernel,
-        out_shape=(
-            jax.ShapeDtypeStruct((2, 3, MX, width), F32),
-            jax.ShapeDtypeStruct((2, 3, rows, LANES), F32),
-            jax.ShapeDtypeStruct((4, 3, MX, LANES), F32),
-        ),
-        in_specs=[anywhere],
-        out_specs=(anywhere,) * 3,
-        scratch_shapes=[pltpu.SemaphoreType.DMA((8,)), pltpu.SemaphoreType.DMA((8,))],
-        compiler_params=pltpu.CompilerParams(collective_id=0, has_side_effects=True),
-    )(perm)
+        for n, (src, dst, target) in enumerate(plans)
+    ]
 
 
 def assemble(own, hx, hy, hc, ext):
@@ -607,12 +586,14 @@
     return [value for value in corners(update)]
 
 
-def greet_groups():
+def greet(plans):
     i = lax.axis_index("gx")
     j = lax.axis_index("gy")
     ni = lax.axis_size("gx")
     nj = lax.axis_size("gy")
     barrier = pltpu.get_barrier_semaphore()
+    for _, _, target in plans:
+        pl.semaphore_signal(barrier, inc=1, device_id=target, device_id_type=MESH)
 
     def greet_y(d, carry):
         pl.semaphore_signal(barrier, inc=1, device_id=(i, lax.rem(j + d, nj)), device_id_type=MESH)
@@ -624,6 +605,7 @@
 
     lax.fori_loop(1, nj, greet_y, 0)
     lax.fori_loop(1, ni, greet_x, 0)
+    pl.semaphore_wait(barrier, ni + nj - 2 + len(plans))
 
 
 def coarse_work(line, rows, block, grid, send1, recv1, send2, recv2):
@@ -631,8 +613,6 @@
     j = lax.axis_index("gy")
     ni = lax.axis_size("gx")
     nj = lax.axis_size("gy")
-    pl.semaphore_wait(pltpu.get_barrier_semaphore(), ni + nj - 2)
-
     def copy_y(d):
         return pltpu.make_async_remote_copy(
             src_ref=line, dst_ref=rows.at[j], send_sem=send1.at[d], recv_sem=recv1.at[d],
@@ -770,15 +750,30 @@
         twin[:, t * LANES:(t + 1) * LANES] = out
 
 
-def solve_kernel(own, hx, hy, hc, matrix, masks, fine, twin, phi_f, phi_t, rows_f, rows_t, line, *scratch):
+def solve_kernel(perm, matrix_in, masks_in, fine, twin, own, hx, hy, hc, matrix, masks, send, recv, fetch,
+                 phi_f, phi_t, rows_f, rows_t, line, *scratch):
     exchange, local = scratch[:7], scratch[7:]
-    greet_groups()
+    plans = halo_plans(perm, hx, hy, hc)
+    fetches = [
+        pltpu.make_async_copy(src, dst, fetch.at[n])
+        for n, (src, dst) in enumerate(((perm, own), (matrix_in, matrix), (masks_in, masks)))
+    ]
+    for copy in fetches:
+        copy.start()
+    greet(plans)
+    copies = halo_copies(plans, send, recv)
+    for copy in copies:
+        copy.start()
+    for copy in fetches:
+        copy.wait()
+    for copy in copies:
+        copy.wait()
     local_work(own, hx, hy, hc, matrix, masks, phi_f, phi_t, line, *local)
     nodes = coarse_work(line, *exchange)
     pressure_work(phi_f, phi_t, nodes, fine, twin, rows_f, rows_t)
 
 
-def solve(perm, hx, hy, hc, ni, nj):
+def solve(perm, ni, nj):
     vmem = pl.BlockSpec(memory_space=pltpu.VMEM)
     return pl.pallas_call(
         solve_kernel,
@@ -786,9 +781,18 @@
             jax.ShapeDtypeStruct((EL, 2048), F32),
             jax.ShapeDtypeStruct((EL // 2, 512), F32),
         ),
-        in_specs=[vmem] * 6,
+        in_specs=[pl.BlockSpec(memory_space=pl.ANY)] * 3,
         out_specs=(vmem, vmem),
         scratch_shapes=[
+            pltpu.VMEM(perm.shape, F32),
+            pltpu.VMEM((2, 3, MX, perm.shape[2]), F32),
+            pltpu.VMEM((2, 3, perm.shape[1], LANES), F32),
+            pltpu.VMEM((4, 3, MX, LANES), F32),
+            pltpu.VMEM((LANES, LANES), jnp.bfloat16),
+            pltpu.VMEM((10, 8, LANES), F32),
+            pltpu.SemaphoreType.DMA((8,)),
+            pltpu.SemaphoreType.DMA((8,)),
+            pltpu.SemaphoreType.DMA((3,)),
             pltpu.VMEM((2, EL, FINE.nk, 8, LANES), F32),
             pltpu.VMEM((EL // 2, TWIN.nk, 8, LANES), F32),
             pltpu.VMEM((2, FINE.nk, EL, LANES), F32),
@@ -806,7 +810,7 @@
             collective_id=1, has_side_effects=True, vmem_limit_bytes=VLIMIT
         ),
     )(
-        perm, hx, hy, hc,
+        perm,
         jnp.asarray(coarsen_matrix(), jnp.bfloat16), jnp.asarray(stencil_masks()),
     )
 
@@ -815,8 +819,7 @@
     ni, nj = mesh.shape["gx"], mesh.shape["gy"]
 
     def shards(perm):
-        hx, hy, hc = halo(perm)
-        return solve(perm, hx, hy, hc, ni, nj)
+        return solve(perm, ni, nj)
 
     return jax.shard_map(
         shards,

time: 63.7 us -> 62 us (0.973)
  Pallas kernels: 60.7 us -> 59 us
    pallas_call x1 -> x0, Pallas kernels: 15.4 us -> none  [halo(): pl.pallas_call(halo_kernel, out_shape=(jax.ShapeDtypeStruct((2, 3, MX, wi...]
    pallas_call x1, Pallas kernels: 45.3 us -> 59 us  [solve(): pl.pallas_call(solve_kernel, out_shape=(jax.ShapeDtypeStruct((EL, 2048),...]
where the time goes in v5:
time: 62 us; the launch traced here: 61.9 us
  Pallas kernels  59 us (95%)
  local copies, waits for them, and re-layouts  2.29 us (4%)
  between operations  0.65 us (1%)
    pallas_call x1, Pallas kernels, solve(): pl.pallas_call(solve_kernel, out_shape=(jax.ShapeDtypeStruct((EL, 2048),...  59 us
    unnamed x4, local copies, waits for them, and re-layouts  2.29 us

profile of v5, /device:TPU:1, one launch (start us, length us, event | category | flops | bytes accessed | tf_op | source)
XLA Modules:
  0.0 61.9 jit_solution(6371154700001519092)
XLA Ops:
  0.6 59.0 %shard_map.50 = (f32[32,2048]{1,0:T(8,128)}, f32[16,512]{1,0:T(8,128)}) custom-call(f32[3,32,2048]{2,1,0:T(8,128)} %perm.1, bf16[128,128]{1,0:T(8,128)(2,1)} %constant.4.clone.matrix_in, f32[10,8,128]{2,1,0:T(8,128)} %constant.5.clone.masks_in), custom_call_target="tpu_custom_call" | custom-call | tf_op jit(solution)/shard_map/pallas_call | solution.py:778
  59.6 0.0 copy-start
  59.6 1.7 %copy.7 = f32[32,2048]{1,0:T(8,128)} copy(f32[32,2048]{1,0:T(8,128)} %get-tuple-element.4) | data formatting | bytes 524288
  61.3 0.0 copy-done
  61.3 0.6 copy.8
Async XLA Ops:
  59.6 1.7 %copy-start = (f32[16,512]{1,0:T(8,128)S(1)}, f32[16,512]{1,0:T(8,128)}, u32[]{:S(2)}) copy-start(f32[16,512]{1,0:T(8,128)} %get-tuple-element.5) | copy-start | bytes 98308

commit v6 on v5

--- a/solution.py
+++ b/solution.py
@@ -608,7 +608,7 @@
     pl.semaphore_wait(barrier, ni + nj - 2 + len(plans))
 
 
-def coarse_work(line, rows, block, grid, send1, recv1, send2, recv2):
+def coarse_work(line, rows, block, grid, send1, recv1, send2, recv2, first_wait, second_wait):
     i = lax.axis_index("gx")
     j = lax.axis_index("gy")
     ni = lax.axis_size("gx")
@@ -643,6 +643,7 @@
 
     lax.fori_loop(1, nj, start_y, 0)
     rows[j] = line[...]
+    first_wait()
     lax.fori_loop(1, nj, wait_y, 0)
     quarter = rows[:, 0, :]
     turned = jnp.transpose(jnp.concatenate([quarter] * 4, axis=0))
@@ -653,80 +654,71 @@
     block[...] = out
     lax.fori_loop(1, ni, start_x, 0)
     grid[pl.ds(pl.multiple_of(i * 16, 16), 16), :] = out
+    second_wait()
     lax.fori_loop(1, ni, wait_x, 0)
     return coarse_solve(lambda q: grid[pl.ds(q, 8, stride=16), :], lane_iota(8))
 
 
-def fold_rows(values, sub):
-    low = sub < 4
-    step = [
-        jnp.where(low, values[n], values[n + 4])
-        + pltpu.roll(jnp.where(low, values[n + 4], values[n]), 4, 0)
-        for n in range(4)
+def turn_rows(values, sub):
+    step = [values]
+    for shift in (4, 2, 1):
+        keep = (sub & shift) == 0
+        after = []
+        for part in step:
+            low, high = [], []
+            for n in range(shift):
+                first, second = part[n], part[n + shift]
+                low.append(jnp.where(keep, first, pltpu.roll(second, shift, 0)))
+                high.append(jnp.where(keep, pltpu.roll(first, 8 - shift, 0), second))
+            after += [low, high]
+        step = after
+    return [part[0] for part in step]
+
+
+def row_sets(phi, sub, lower):
+    rows = turn_rows(phi, sub)
+    base = (rows[0] + rows[2]) + (rows[4] + rows[6])
+    return [jnp.where(lower, base, 0.0)] + [
+        jnp.where(lower, rows[2 * a + 1], rows[2 * a]) for a in range(4)
     ]
-    for shift in (2, 1):
-        keep = (sub & shift) == 0
-        step = [
-            jnp.where(
-                keep,
-                step[n] + pltpu.roll(step[n], 8 - shift, 0),
-                step[n + shift] + pltpu.roll(step[n + shift], shift, 0),
-            )
-            for n in range(shift)
-        ]
-    return step[0]
-
-
-def pressure_work(phi_f, phi_t, nodes, fine, twin, rows_f, rows_t):
-    i = lax.axis_index("gx")
-    j = lax.axis_index("gy")
+
+
+def prepare_rows(phi_f, phi_t, rows_f, rows_t):
     sub = lax.broadcasted_iota(jnp.int32, (8, LANES), 0)
     lane = lane_iota(8)
-    corner, az = sub >> 1, (sub & 1) == 1
-
-    def own_nodes(level, col):
-        here = (sub == i) & (lane == level * 64 + col * 32 + j)
-        out = jnp.zeros((8, LANES), F32)
-        for a in range(4):
-            value = jnp.where(here, nodes[a], 0.0)
-            value = jnp.sum(jnp.sum(value, axis=0, keepdims=True), axis=1, keepdims=True)
-            out = jnp.where(corner == a, value, out)
-        return jnp.where(az, out, 1.0), jnp.where(az, 0.0, out)
-
     _, seg, _ = split_lane(FINE, lane)
-    fine_weights = []
-    for col in range(2):
-        first, second = own_nodes(0, col)
-        fine_weights.append(jnp.where(seg == 0, first, second))
+    lower_f = seg == 0
     _, seg, _ = split_lane(TWIN, lane)
-    twin_weights = jnp.zeros((8, LANES), F32)
-    for col in range(2):
-        first, second = own_nodes(1, col)
-        twin_weights = jnp.where(seg == 2 * col, first, twin_weights)
-        twin_weights = jnp.where(seg == 2 * col + 1, second, twin_weights)
+    lower_t = (seg == 0) | (seg == 2)
 
     def fine_rows(k, carry):
         for col in range(2):
             for g in range(EL // 8):
-                values = [phi_f[col, 8 * g + n, k] * fine_weights[col] for n in range(8)]
-                rows_f[col, k, 8 * g:8 * g + 8, :] = fold_rows(values, sub)
+                sets = row_sets([phi_f[col, 8 * g + n, k] for n in range(8)], sub, lower_f)
+                for n in range(5):
+                    rows_f[n, col, k, 8 * g:8 * g + 8, :] = sets[n]
         return carry
 
     lax.fori_loop(0, FINE.nk, fine_rows, 0)
 
     def twin_rows(k, carry):
         for g in range(EL // 16):
-            values = [phi_t[8 * g + n, k] * twin_weights for n in range(8)]
-            rows_t[k, 8 * g:8 * g + 8, :] = fold_rows(values, sub)
+            sets = row_sets([phi_t[8 * g + n, k] for n in range(8)], sub, lower_t)
+            for n in range(5):
+                rows_t[n, k, 8 * g:8 * g + 8, :] = sets[n]
         return carry
 
     lax.fori_loop(0, TWIN.nk, twin_rows, 0)
 
-    def turn(value, shift):
-        return pltpu.roll(value, shift % LANES, 1) if shift % LANES else value
-
+
+def turn(value, shift):
+    return pltpu.roll(value, shift % LANES, 1) if shift % LANES else value
+
+
+def lay_out_fine(rows_f, sets_f, col):
     wide = lane_iota(EL)
-    for col in range(2):
+
+    def body(n, carry):
         for t in range(8):
             out = None
             for h in range(4):
@@ -734,24 +726,55 @@
                 c, k = y // FINE.nk, y % FINE.nk
                 for e in range(2):
                     to = h * 32 + e * 16
-                    piece = turn(rows_f[col, k], to - (c * GROUP + e * 20 + MZ))
+                    piece = turn(rows_f[n, col, k], to - (c * GROUP + e * 20 + MZ))
                     out = piece if out is None else jnp.where(wide >= to, piece, out)
-            fine[:, (col * 8 + t) * LANES:(col * 8 + t + 1) * LANES] = out
+            sets_f[n, col * 8 + t] = out
+        return carry
+
+    lax.fori_loop(0, 5, body, 0)
+
+
+def lay_out_twin(rows_t, sets_t):
     wide = lane_iota(EL // 2)
-    for t in range(4):
-        out = None
-        for h in range(8):
-            col, y = (8 * t + h) // 16, (8 * t + h) % 16 + MX // 2
-            c, k = y // TWIN.nk, y % TWIN.nk
-            for e in range(2):
-                to = h * 16 + e * 8
-                piece = turn(rows_t[k], to - (c * GROUP + col * 20 + e * 10 + MZ // 2))
-                out = piece if out is None else jnp.where(wide >= to, piece, out)
-        twin[:, t * LANES:(t + 1) * LANES] = out
+
+    def body(n, carry):
+        for t in range(4):
+            out = None
+            for h in range(8):
+                col, y = (8 * t + h) // 16, (8 * t + h) % 16 + MX // 2
+                c, k = y // TWIN.nk, y % TWIN.nk
+                for e in range(2):
+                    to = h * 16 + e * 8
+                    piece = turn(rows_t[n, k], to - (c * GROUP + col * 20 + e * 10 + MZ // 2))
+                    out = piece if out is None else jnp.where(wide >= to, piece, out)
+            sets_t[n, t] = out
+        return carry
+
+    lax.fori_loop(0, 5, body, 0)
+
+
+def combine(nodes, sets_f, sets_t, fine, twin):
+    i = lax.axis_index("gx")
+    j = lax.axis_index("gy")
+    sub = lax.broadcasted_iota(jnp.int32, (8, LANES), 0)
+    lane = lane_iota(8)
+    for level in range(2):
+        for col in range(2):
+            here = (sub == i) & (lane == level * 64 + col * 32 + j)
+            weights = []
+            for a in range(4):
+                value = jnp.sum(jnp.where(here, nodes[a], 0.0), axis=0, keepdims=True)
+                weights.append(jnp.sum(value, axis=1, keepdims=True))
+            sets, out, count = (sets_t, twin, 2) if level else (sets_f, fine, 8)
+            for t in range(col * count, (col + 1) * count):
+                total = sets[0, t]
+                for a in range(4):
+                    total = total + weights[a] * sets[a + 1, t]
+                out[:, t * LANES:(t + 1) * LANES] = total
 
 
 def solve_kernel(perm, matrix_in, masks_in, fine, twin, own, hx, hy, hc, matrix, masks, send, recv, fetch,
-                 phi_f, phi_t, rows_f, rows_t, line, *scratch):
+                 phi_f, phi_t, rows_f, rows_t, sets_f, sets_t, line, *scratch):
     exchange, local = scratch[:7], scratch[7:]
     plans = halo_plans(perm, hx, hy, hc)
     fetches = [
@@ -769,8 +792,17 @@
     for copy in copies:
         copy.wait()
     local_work(own, hx, hy, hc, matrix, masks, phi_f, phi_t, line, *local)
-    nodes = coarse_work(line, *exchange)
-    pressure_work(phi_f, phi_t, nodes, fine, twin, rows_f, rows_t)
+
+    def first_wait():
+        prepare_rows(phi_f, phi_t, rows_f, rows_t)
+        lay_out_fine(rows_f, sets_f, 0)
+
+    def second_wait():
+        lay_out_fine(rows_f, sets_f, 1)
+        lay_out_twin(rows_t, sets_t)
+
+    nodes = coarse_work(line, *exchange, first_wait, second_wait)
+    combine(nodes, sets_f, sets_t, fine, twin)
 
 
 def solve(perm, ni, nj):
@@ -795,8 +827,10 @@
             pltpu.SemaphoreType.DMA((3,)),
             pltpu.VMEM((2, EL, FINE.nk, 8, LANES), F32),
             pltpu.VMEM((EL // 2, TWIN.nk, 8, LANES), F32),
-            pltpu.VMEM((2, FINE.nk, EL, LANES), F32),
-            pltpu.VMEM((TWIN.nk, EL // 2, LANES), F32),
+            pltpu.VMEM((5, 2, FINE.nk, EL, LANES), F32),
+            pltpu.VMEM((5, TWIN.nk, EL // 2, LANES), F32),
+            pltpu.VMEM((5, 16, EL, LANES), F32),
+            pltpu.VMEM((5, 4, EL // 2, LANES), F32),
             pltpu.VMEM((1, LANES), F32),
             pltpu.VMEM((nj, 1, LANES), F32),
             pltpu.VMEM((16, LANES), F32),

time: 62 us -> 60.8 us (0.981)
  Pallas kernels: 59 us -> 57.8 us
    pallas_call x1, Pallas kernels: 59 us -> 57.8 us  [solve(): pl.pallas_call(solve_kernel, out_shape=(jax.ShapeDtypeStruct((EL, 2048),...]
where the time goes in v6:
time: 60.8 us
  Pallas kernels  57.8 us (95%)
  local copies, waits for them, and re-layouts  2.29 us (4%)
  between operations  0.65 us (1%)
    pallas_call x1, Pallas kernels, solve(): pl.pallas_call(solve_kernel, out_shape=(jax.ShapeDtypeStruct((EL, 2048),...  57.8 us
    unnamed x4, local copies, waits for them, and re-layouts  2.29 us

profile of v6, /device:TPU:1, one launch (start us, length us, event | category | flops | bytes accessed | tf_op | source)
XLA Modules:
  0.0 60.8 jit_solution(318564354441821879)
XLA Ops:
  0.6 57.8 %shard_map.50 = (f32[32,2048]{1,0:T(8,128)}, f32[16,512]{1,0:T(8,128)}) custom-call(f32[3,32,2048]{2,1,0:T(8,128)} %perm.1, bf16[128,128]{1,0:T(8,128)(2,1)} %constant.4.clone.matrix_in, f32[10,8,128]{2,1,0:T(8,128)} %constant.5.clone.masks_in), custom_call_target="tpu_custom_call" | custom-call | tf_op jit(solution)/shard_map/pallas_call | solution.py:810
  58.4 0.0 copy-start
  58.5 1.7 %copy.7 = f32[32,2048]{1,0:T(8,128)} copy(f32[32,2048]{1,0:T(8,128)} %get-tuple-element.4) | data formatting | bytes 524288
  60.1 0.0 copy-done
  60.1 0.6 %copy.8 = f32[16,512]{1,0:T(8,128)} copy(f32[16,512]{1,0:T(8,128)S(1)} %copy-done) | data formatting | bytes 65536
Async XLA Ops:
  58.4 1.7 %copy-start = (f32[16,512]{1,0:T(8,128)S(1)}, f32[16,512]{1,0:T(8,128)}, u32[]{:S(2)}) copy-start(f32[16,512]{1,0:T(8,128)} %get-tuple-element.5) | copy-start | bytes 98308
